TPU v7x, 32 devices: a whole 2x2x4 slice. The times are simulated.
32 devices in a mesh: grp: 2 (over y), epoch: 4 (over x, core), asset: 4 (over z).
Axes of the slice: x: 2, y: 2, z: 4, core: 2. Of those that a mesh axis runs over, the one named last changes fastest.
Arguments:
- signals: bfloat16 [8, 1024, 256], P(('grp', 'epoch'), 'asset'), parts along dimension 0, may hold values from -6 to 6
- targets: bfloat16 [8, 1024, 256], P(('grp', 'epoch'), 'asset'), parts along dimension 0, may hold values from -6 to 6
- row_counts: int32 [8, 4], P(('grp', 'epoch'), 'asset'), parts along dimension 0, may hold values from 32 to 256, as said below
- feature_weights: bfloat16 [256, 2048], replicated, may hold values from -0.375 to 0.375
- phases: float32 [2048], replicated, may hold values from -3.140625 to 3.140625
- spread_ids: int32 [2048], replicated, may hold values from 0 to 3
Outputs:
- coefficients: float32 [8, 2048, 256], P(('grp', 'epoch'), 'asset'), parts along dimension 0
There are 2 independent parts, one for each index of `grp`. A program takes and returns all parts, laid end to end along the dimension named above; an argument that names none is the same for every part. Nothing has to cross between parts.
Inputs may be any that keep to these rules, and one draw needn't show every extreme that they name: `row_counts`: each count is at least 32, and in every epoch some asset group has exactly 256 live rows.
All inputs are finite; a program needn't handle non-finite values.
Results may differ from a plain program's by a relative error of at most 0.0003.
Values may be sent and summed in bfloat16 or wider, within the bound.
No kernel may reach another device: no remote copies, remote signals or barrier semaphores. Data moves between devices by JAX's collectives and lax.ppermute only.
A program may use at most 64 MiB of HBM per device.

v0:
```python
import jax
import jax.numpy as jnp
from jax import lax
from jax.sharding import PartitionSpec as P

ITERS = 3


ridge_penalty = 0.05
epsilon = 1e-06


def prefix(part, axis, combine, identity):
    place = lax.axis_index(axis)
    gathered = jax.tree.map(lambda a: lax.all_gather(a, axis), part)
    state = jax.tree.map(lambda a, e: jnp.zeros_like(a) + jnp.asarray(e, a.dtype), part, identity)

    def one(hop, state):
        return combine(
            state, jax.tree.map(lambda a: lax.dynamic_index_in_dim(a, hop, 0, False), gathered)
        )

    return lax.fori_loop(0, place, one, state)


def feature_scale(spread_ids):
    return (
        0.5
        * (
            1.0
            + jnp.where(spread_ids >= 1, 1.0, 0.0)
            + jnp.where(spread_ids >= 2, 2.0, 0.0)
            + jnp.where(spread_ids >= 3, 4.0, 0.0)
        )
    ).astype(jnp.float32)


def make_features(inputs, feature_weights, phases, spread_ids):
    projected = jnp.dot(inputs, feature_weights, preferred_element_type=jnp.float32)
    return jnp.sin(projected * feature_scale(spread_ids) + phases)


def add_pair(earlier, later):
    return (earlier[0] + later[0], earlier[1] + later[1])


def on_device(signals, targets, row_counts, feature_weights, phases, spread_ids):
    rows = signals.shape[1]
    width = feature_weights.shape[1]
    tgt_width = targets.shape[2]
    groups = lax.axis_size("asset")
    block_size = width // groups
    entries = width * tgt_width
    own_rows = row_counts[0, 0]
    all_counts = lax.all_gather(row_counts[0], "asset", axis=0, tiled=True)
    row_sum = jnp.sum(all_counts).astype(jnp.float32)
    inputs = signals[0]
    returns = targets[0]
    features = make_features(inputs, feature_weights, phases, spread_ids)
    live_mask = (jnp.arange(rows) < own_rows)[:, None]
    features = jnp.where(live_mask, features, jnp.zeros_like(features))
    returns = jnp.where(live_mask, returns.astype(jnp.float32), jnp.zeros((), jnp.float32))
    combined = jnp.concatenate([features, returns], axis=1)
    contract_rows = (((0,), (0,)), ((), ()))
    gram_block = lax.psum_scatter(
        lax.dot_general(features, combined, contract_rows, precision=lax.Precision.HIGHEST),
        "asset",
        scatter_dimension=0,
        tiled=True,
    )
    earlier, earlier_rows = prefix(
        (gram_block, row_sum),
        "epoch",
        add_pair,
        (jnp.zeros_like(gram_block), jnp.zeros((), jnp.float32)),
    )
    cumulative = earlier + gram_block
    row_total = earlier_rows + row_sum
    first_row = lax.axis_index("asset") * block_size
    diagonal = jnp.arange(width)[None, :] == first_row + jnp.arange(block_size)[:, None]
    system = cumulative[:, :width] / row_total + ridge_penalty * jnp.where(
        diagonal, 1.0, 0.0
    ).astype(jnp.float32)
    residual = cumulative[:, width:] / row_total
    coef = jnp.zeros((block_size, tgt_width), jnp.float32)
    for iteration in range(ITERS):
        image = jnp.zeros((block_size, tgt_width), jnp.float32) + jnp.dot(
            system,
            lax.all_gather(residual, "asset", axis=0, tiled=True),
            precision=lax.Precision.HIGHEST,
        )
        res_norm, res_curve = lax.psum(
            (jnp.sum(residual * residual), jnp.sum(residual * image)), "asset"
        )
        step_size = res_norm / entries / (res_curve / entries + epsilon)
        coef = coef + step_size * residual
        residual = residual - step_size * image
    return (jnp.sqrt(row_total) * coef)[None]


def solution(mesh):
    placed = (
        P(("grp", "epoch"), "asset", None),
        P(("grp", "epoch"), "asset", None),
        P(("grp", "epoch"), "asset"),
        P(),
        P(),
        P(),
    )
    return jax.shard_map(
        on_device,
        mesh=mesh,
        in_specs=placed,
        out_specs=P(("grp", "epoch"), "asset", None),
        check_vma=False,
    )
```

profile of v0, /device:TPU:7, one launch (start us, length us, event | category | flops | bytes accessed | tf_op | source)
XLA Modules:
  0.0 706.8 jit_solution(8003672284095175270)
XLA Ops:
  7.3 0.7 add_multiply_fusion
  8.0 1.0 convert_select_fusion
  9.0 8.1 %fusion.3 = f32[256,2048]{1,0:T(8,128)S(1)} fusion(bf16[256,2048]{1,0:T(8,128)(2,1)S(1)} %copy-done, f32[2048]{0:T(1024)} %param.12, f32[2048]{0:T(1024)S(1)} %add_multiply_fusion, pred[256]{0:T(512)(128)(4,1)S(1)} %iota_compare_fusion.1, bf16[1,256,256]{2,1,0:T(8,128)(2,1)} %param.8), kind=kOutput, calls=%fused_computation.7 | convolution fusion | flops 270008320 | bytes 3293440 | tf_op jit(solution)/shard_map/dot_general | solution.py:39
  17.1 19.4 %fusion.4 = f32[2048,2304]{1,0:T(8,128)} fusion(f32[256,2048]{1,0:T(8,128)S(1)} %fusion.3, f32[256,256]{1,0:T(8,128)S(1)} %convert_select_fusion), kind=kOutput, calls=%fused_computation.8 | convolution fusion | flops 14496104448 | bytes 21233664 | tf_op jit(solution)/shard_map/dot_general | solution.py:66
  36.6 314.8 %reduce-scatter.2.cloned.1.call-done = f32[512,2304]{1,0:T(8,128)} async-done(((f32[2048,2304]{1,0:T(8,128)}), f32[512,2304]{1,0:T(8,128)}) %reduce-scatter.2.cloned.1.call-update) | async-done | bytes 4718608 | tf_op jit(solution)/shard_map/reduce_scatter | solution.py:65
  352.7 7.6 %all-reduce = s32[4]{0:T(128)S(1)} all-reduce(s32[4]{0:T(128)S(1)} %bitcast_dynamic-update-slice_fusion), channel_id=3, replica_groups=mesh['grp'=2,'epoch'=4,'asset'=4] {'asset'}, use_global_device_ids=true, to_apply=%add | all-reduce | flops 4 | bytes 32
  362.2 0.8 dynamic-update-slice.1
  362.9 7.8 %all-reduce.1 = f32[4]{0:T(128)S(1)} all-reduce(f32[4]{0:T(128)S(1)} %dynamic-update-slice.1), channel_id=1, replica_groups=mesh['grp'=2,'epoch'=4,'asset'=4] {'epoch'}, use_global_device_ids=true, to_apply=%add.1 | all-reduce | flops 4 | bytes 32
  370.7 103.2 %all-gather.13.cloned.1.call-done = f32[2048,2304]{1,0:T(8,128)} async-done(((f32[512,2304]{1,0:T(8,128)}), f32[2048,2304]{1,0:T(8,128)}) %all-gather.13.cloned.1.call-update) | async-done | bytes 18874384 | tf_op jit(solution)/shard_map/all_gather | solution.py:15
  473.9 2.5 broadcast_in_dim.58
  476.4 23.6 %while.12 = (s32[]{:T(128)}, f32[512,2304]{1,0:T(8,128)}, f32[]{:T(128)}, s32[]{:T(128)}, f32[4,512,2304]{2,1,0:T(8,128)}, /*index=5*/f32[4]{0:T(128)S(1)}, s32[]{:T(128)}, s32[]{:T(128)}, s32[]{:T(128)}) while((s32[]{:T(128)}, f32[512,2304]{1,0:T(8,128)}, f32[]{:T(128)}, s32[]{:T(128)}, f32[4,512,2304]{2,1,0:T(8,128)}, ...), condition=%wide.region_3.4_spmd, body=%wide.region_2.3_spmd.sunk | while | flops 1179654 | bytes 14155931 | solution.py:23
  476.4 6.6 bitcast_add_fusion.2
  483.0 0.6 dynamic_slice.12
  484.3 6.6 bitcast_add_fusion.2
  492.2 6.6 bitcast_add_fusion.2
  498.8 0.6 dynamic_slice.12
  500.1 4.3 add.88
  504.4 2.1 copy-done.2
  506.5 0.8 slice_divide_fusion.1
  507.4 5.1 fusion
  512.6 40.8 %all-gather.7.cloned.1.call-done = f32[2048,256]{1,0:T(8,128)} async-done(((f32[512,256]{1,0:T(8,128)}), f32[2048,256]{1,0:T(8,128)}) %all-gather.7.cloned.1.call-update) | async-done | bytes 2097168 | tf_op jit(solution)/shard_map/all_gather | solution.py:89
  553.4 6.6 multiply_reduce_fusion.3
  560.0 8.4 %all-reduce.4 = (f32[]{:T(128)}, f32[]{:T(128)}) all-reduce(f32[]{:T(128)} %get-tuple-element.44, f32[]{:T(128)} %get-tuple-element.43), channel_id=1, replica_groups=mesh['grp'=2,'epoch'=4,'asset'=4] {'asset'}, use_global_device_ids=true, to_apply=%region_5.6 | all-reduce | flops 2 | bytes 16 | tf_op jit(solution)/shard_map/psum | solution.py:92
  569.7 1.9 multiply_subtract_fusion.1
  571.9 45.7 %all-gather.9.cloned.1.call-done = f32[2048,256]{1,0:T(8,128)} async-done(((f32[512,256]{1,0:T(8,128)}), f32[2048,256]{1,0:T(8,128)}) %all-gather.9.cloned.1.call-update) | async-done | bytes 2097168 | tf_op jit(solution)/shard_map/all_gather | solution.py:89
  617.6 6.9 multiply_reduce_fusion.1
  624.6 8.5 %all-reduce.3 = (f32[]{:T(128)}, f32[]{:T(128)}) all-reduce(f32[]{:T(128)} %get-tuple-element.42, f32[]{:T(128)} %get-tuple-element.41), channel_id=1, replica_groups=mesh['grp'=2,'epoch'=4,'asset'=4] {'asset'}, use_global_device_ids=true, to_apply=%region_9.10 | all-reduce | flops 2 | bytes 16 | tf_op jit(solution)/shard_map/psum | solution.py:92
  634.4 1.4 multiply_reduce_fusion
  635.9 45.9 %all-gather.11.cloned.1.call-done = f32[2048,256]{1,0:T(8,128)} async-done(((f32[512,256]{1,0:T(8,128)}), f32[2048,256]{1,0:T(8,128)}) %all-gather.11.cloned.1.call-update) | async-done | bytes 2097168 | tf_op jit(solution)/shard_map/all_gather | solution.py:89
  681.8 6.9 fusion.8
  688.7 8.4 %all-reduce.2 = (f32[]{:T(128)}, f32[]{:T(128)}) all-reduce(f32[]{:T(128)} %get-tuple-element.63, f32[]{:T(128)} %fusion.8), channel_id=1, replica_groups=mesh['grp'=2,'epoch'=4,'asset'=4] {'asset'}, use_global_device_ids=true, to_apply=%region_13.14 | all-reduce | flops 2 | bytes 16 | tf_op jit(solution)/shard_map/psum | solution.py:92
  698.4 2.0 multiply_bitcast_fusion
  (34 shorter events, 3.6 us)
Async XLA Ops:
  6.5 2.5 copy-start
  6.5 344.9 %reduce-scatter.2.cloned.1.call-start = ((), (), s32[]{:S(2)}) async-start(), calls=%async_computation.1 | async-start | bytes 23592960 | tf_op jit(solution)/shard_map/reduce_scatter | solution.py:65
  36.5 315.0 %copy-start.7 = (u32[32]{0:T(128)S(1)}, u32[32]{0:T(128)}, u32[]{:S(2)}) copy-start(u32[32]{0:T(128)} %constant.59) | copy-start | bytes 388
  36.6 325.0 %copy-start.6 = (u32[32]{0:T(128)S(1)}, u32[32]{0:T(128)}, u32[]{:S(2)}) copy-start(u32[32]{0:T(128)} %constant.64) | copy-start | bytes 388
  36.6 437.3 %all-gather.13.cloned.1.call-start = ((), (), s32[]{:S(2)}) async-start(), calls=%async_computation.5 | async-start | bytes 23592960 | tf_op jit(solution)/shard_map/all_gather | solution.py:15
  351.4 201.9 %all-gather.7.cloned.1.call-start = ((), (), s32[]{:S(2)}) async-start(), calls=%async_computation.2 | async-start | bytes 2621440 | tf_op jit(solution)/shard_map/all_gather | solution.py:89
  504.4 2.1 copy-start.2
  507.4 110.3 %all-gather.9.cloned.1.call-start = ((), (), s32[]{:S(2)}) async-start(), calls=%async_computation.3 | async-start | bytes 2621440 | tf_op jit(solution)/shard_map/all_gather | solution.py:89
  507.4 45.9 %copy-start.5 = (f32[512,256]{1,0:T(8,128)S(1)}, f32[512,256]{1,0:T(8,128)}, u32[]{:S(2)}) copy-start(f32[512,256]{1,0:T(8,128)} %slice_divide_fusion.1) | copy-start | bytes 1572868
  571.6 62.7 %copy-start.3 = (f32[512,256]{1,0:T(8,128)S(1)}, f32[512,256]{1,0:T(8,128)}, u32[]{:S(2)}) copy-start(f32[512,256]{1,0:T(8,128)} %multiply_subtract_fusion.1) | copy-start | bytes 1572868
  571.7 110.1 %all-gather.11.cloned.1.call-start = ((), (), s32[]{:S(2)}) async-start(), calls=%async_computation.4 | async-start | bytes 2621440 | tf_op jit(solution)/shard_map/all_gather | solution.py:89
  635.8 62.6 %copy-start.4 = (f32[512,256]{1,0:T(8,128)S(1)}, f32[512,256]{1,0:T(8,128)}, u32[]{:S(2)}) copy-start(f32[512,256]{1,0:T(8,128)} %get-tuple-element.64) | copy-start | bytes 1572868
  635.8 64.5 %copy-start.1 = (bf16[256,2048]{1,0:T(8,128)(2,1)S(1)}, bf16[256,2048]{1,0:T(8,128)(2,1)}, u32[]{:S(2)}) copy-start(bf16[256,2048]{1,0:T(8,128)(2,1)} %param.11) | copy-start | bytes 3145732
Sparse Core Ops, SparseCore 0:
  36.7 314.7 reduce-scatter.1
  353.0 120.8 all-gather.12
  507.5 45.8 all-gather.6
  571.8 45.8 all-gather.8
  635.9 45.8 all-gather.10
where the time goes:
time: 711 us; the launch traced here: 707 us
  waiting for transfers between devices  550 us (77%)
  matrix products  48 us (7%)
  blocking collectives  40.6 us (6%)
  other arithmetic  37.6 us (5%)
  between operations  18.6 us (3%)
  local copies, waits for them, and re-layouts  9.17 us (1%)
    reduce_scatter x1, waiting for transfers between devices, on_device(): lax.psum_scatter(lax.dot_general(features, combined, contract_rows, preci...  315 us
    all_gather x3, waiting for transfers between devices, on_device(): lax.all_gather(residual, 'asset', axis=0, tiled=True)  132 us
    all_gather x1, waiting for transfers between devices, prefix(): gathered = jax.tree.map(lambda a: lax.all_gather(a, axis), part)  103 us
    psum x3, blocking collectives, on_device(): lax.psum((jnp.sum(residual * residual), jnp.sum(residual * image)), 'asset')  25.3 us
    dot_general x3, matrix products, on_device(): jnp.dot(system, lax.all_gather(residual, 'asset', axis=0, tiled=True), pr...  20.5 us
    add x3, other arithmetic, add_pair(): return (earlier[0] + later[0], earlier[1] + later[1])  19.7 us
    dot_general x1, matrix products, on_device(): lax.dot_general(features, combined, contract_rows, precision=lax.Precisio...  19.4 us
    unnamed x2, blocking collectives  15.4 us
  transfers between devices with their start and end apart: 5, of which 5 were waited for; matrix products, arithmetic and copies ran while one was open for 1% of the time, Pallas kernels for 0%

commit v1 on v0

--- a/solution.py
+++ b/solution.py
@@ -1,6 +1,8 @@
 import jax
 import jax.numpy as jnp
 from jax import lax
+from jax.experimental import pallas as pl
+from jax.experimental.pallas import tpu as pltpu
 from jax.sharding import PartitionSpec as P
 
 ITERS = 3
@@ -8,6 +10,24 @@
 
 ridge_penalty = 0.05
 epsilon = 1e-06
+
+CHUNK = 256
+TILE = 256
+PACK = 16
+SHARED = 8
+SUBLANES = 16
+LANES = 128
+TURN = 0.15915494309189535
+SINE = (
+    6.283182818537488,
+    -41.34142139758713,
+    81.59618384799899,
+    -76.58010029406394,
+    41.20539392705353,
+    -12.27126097383172,
+)
+NT = (((1,), (1,)), ((), ()))
+NN = (((1,), (0,)), ((), ()))
 
 
 def prefix(part, axis, combine, identity):
@@ -44,7 +64,7 @@
     return (earlier[0] + later[0], earlier[1] + later[1])
 
 
-def on_device(signals, targets, row_counts, feature_weights, phases, spread_ids):
+def gram_form(signals, targets, row_counts, feature_weights, phases, spread_ids):
     rows = signals.shape[1]
     width = feature_weights.shape[1]
     tgt_width = targets.shape[2]
@@ -98,6 +118,423 @@
     return (jnp.sqrt(row_total) * coef)[None]
 
 
+def dot(a, b, dims):
+    return lax.dot_general(a, b, dims, preferred_element_type=jnp.float32)
+
+
+def split(a):
+    high = a.astype(jnp.bfloat16)
+    return high, (a - high.astype(jnp.float32)).astype(jnp.bfloat16)
+
+
+def sine_of_turns(turns):
+    fraction = turns - jnp.round(turns)
+    square = fraction * fraction
+    value = SINE[-1]
+    for c in SINE[-2::-1]:
+        value = value * square + c
+    return value * fraction
+
+
+def kernel_call(kernel, out_shape, in_specs, out_specs, scratch, cost=None):
+    return pl.pallas_call(
+        kernel,
+        out_shape=out_shape,
+        in_specs=in_specs,
+        out_specs=out_specs,
+        scratch_shapes=scratch,
+        cost_estimate=cost,
+        compiler_params=pltpu.CompilerParams(vmem_limit_bytes=60 * 2**20),
+    )
+
+
+WHOLE = pl.BlockSpec(memory_space=pltpu.VMEM)
+SCALARS = pl.BlockSpec(memory_space=pltpu.SMEM)
+REMOTE = pl.BlockSpec(memory_space=pl.ANY)
+
+
+def rows_of(c):
+    return pl.ds(pl.multiple_of(c * CHUNK, CHUNK), CHUNK)
+
+
+def pack_rows(sources, rows, mark, x_buf, y_buf):
+    lane = lax.broadcasted_iota(jnp.int32, (1, LANES), 1)
+    counts = []
+    for x_ref, y_ref, use in sources:
+        for first in range(0, x_ref.shape[0], rows):
+            marks = jnp.sum(y_ref[first : first + rows, :].astype(jnp.float32), axis=0, keepdims=True)
+            counts.append(jnp.sum(jnp.where(lane == mark, marks, 0.0)).astype(jnp.int32) * use)
+    filled = jnp.int32(0)
+    count = jnp.int32(0)
+    place = 0
+    for x_ref, y_ref, use in sources:
+        for first in range(0, x_ref.shape[0], rows):
+            own = counts[place]
+            place += 1
+            at = pl.ds(pl.multiple_of(filled, PACK), rows)
+            x_buf[at, :] = x_ref[first : first + rows, :]
+            y_buf[at, :] = y_ref[first : first + rows, :]
+            count = count + own
+            filled = filled + (own + PACK - 1) // PACK * PACK
+    end = pl.ds(pl.multiple_of(filled, PACK), CHUNK)
+    x_buf[end, :] = jnp.zeros((CHUNK, x_buf.shape[1]), x_buf.dtype)
+    y_buf[end, :] = jnp.zeros((CHUNK, LANES), y_buf.dtype)
+    return (filled + CHUNK - 1) // CHUNK, count
+
+
+def featurize_chunk(x, y, lines, w_ref, ph_ref, cross_ref, put):
+    returns = y[:lines].astype(jnp.bfloat16)
+    for j in range(0, w_ref.shape[1], TILE):
+        js = slice(j, j + TILE)
+        turns = dot(x, w_ref[:, js], NN) * TURN + ph_ref[:, js]
+        high, low = split(sine_of_turns(turns))
+        put(js, high, low)
+        cross_ref[:, js] += dot(returns, high, NN) + dot(returns, low, NN)
+
+
+def near_kernel(sources, rows, lines, mark, use_ref, *refs):
+    x_refs, y_refs = refs[:sources], refs[sources : 2 * sources]
+    w_ref, ph_ref, high_hbm, low_hbm, cross_ref, live_ref, info_ref = refs[2 * sources : 2 * sources + 7]
+    x_buf, y_buf, high_buf, low_buf, high_sem, low_sem = refs[2 * sources + 7 :]
+    sets = [(x_refs[s], y_refs[s], use_ref[s]) for s in range(sources)]
+    chunks, count = pack_rows(sets, rows, mark, x_buf, y_buf)
+    info_ref[0] = chunks
+    info_ref[1] = count
+    cross_ref[...] = jnp.zeros_like(cross_ref)
+
+    def send(c, slot):
+        return (
+            pltpu.make_async_copy(high_buf.at[slot], high_hbm.at[rows_of(c), :], high_sem.at[slot]),
+            pltpu.make_async_copy(low_buf.at[slot], low_hbm.at[rows_of(c), :], low_sem.at[slot]),
+        )
+
+    def one(c, _):
+        slot = lax.rem(c, 2)
+
+        @pl.when(c >= 2)
+        def _():
+            for copy in send(c - 2, slot):
+                copy.wait()
+
+        turned = y_buf[rows_of(c), :].astype(jnp.float32).T
+        live_ref[c] = turned[mark : mark + 8]
+
+        def put(js, high, low):
+            high_buf[slot, :, js] = high
+            low_buf[slot, :, js] = low
+
+        featurize_chunk(x_buf[rows_of(c), :], turned, lines, w_ref, ph_ref, cross_ref, put)
+        for copy in send(c, slot):
+            copy.start()
+        return 0
+
+    lax.fori_loop(0, chunks, one, 0)
+    for back in (2, 1):
+
+        @pl.when(chunks >= back)
+        def _():
+            for copy in send(chunks - back, lax.rem(chunks - back, 2)):
+                copy.wait()
+
+
+def estimate(cols, r, i):
+    f32 = jnp.float32
+    norm = jnp.full((1, 1), jnp.sum(r[cols : cols + SHARED] * r[cols : cols + SHARED]), f32)
+    curve = jnp.full((1, 1), jnp.sum(r[cols : cols + SHARED] * i[cols : cols + SHARED]), f32)
+    good = jnp.logical_and(norm > 0.0, curve > ridge_penalty * 0.5 * norm)
+    return jnp.where(good, norm / jnp.where(good, curve, 1.0), 1.0)
+
+
+def main_kernel(sources, rows, lines, cols, mark, use_ref, info_ref, *refs):
+    x_refs, y_refs = refs[:sources], refs[sources : 2 * sources]
+    w_ref, ph_ref, near_cross, near_live, near_high, near_low = refs[2 * sources : 2 * sources + 6]
+    v0_ref, q1_ref, q2_ref, mom_ref = refs[2 * sources + 6 : 2 * sources + 10]
+    x_buf, y_buf, phi, plo, live, stack, inner, acc, v0, image, q1, high_sem, low_sem = refs[2 * sources + 10 :]
+    f32, bf16 = jnp.float32, jnp.bfloat16
+
+    near = info_ref[0]
+
+    def begin(c, _):
+        at = rows_of(c)
+        pltpu.make_async_copy(near_high.at[at, :], phi.at[at, :], high_sem.at[c]).start()
+        pltpu.make_async_copy(near_low.at[at, :], plo.at[at, :], low_sem.at[c]).start()
+        live[c] = near_live[c]
+        return 0
+
+    lax.fori_loop(0, near, begin, 0)
+    sets = [(x_refs[s], y_refs[s], use_ref[s]) for s in range(sources)]
+    far, count = pack_rows(sets, rows, mark, x_buf, y_buf)
+    chunks = near + far
+    total = (info_ref[1] + count).astype(f32)
+    inverse = 1.0 / jnp.full((1, 1), total, f32)
+
+    v0[...] = near_cross[...]
+
+    def featurize(c, _):
+        turned = y_buf[rows_of(c), :].astype(f32).T
+        live[near + c] = turned[mark : mark + 8]
+        at = rows_of(near + c)
+
+        def put(js, high, low):
+            phi[at, js] = high
+            plo[at, js] = low
+
+        featurize_chunk(x_buf[rows_of(c), :], turned, lines, w_ref, ph_ref, v0, put)
+        return 0
+
+    lax.fori_loop(0, far, featurize, 0)
+
+    def end(c, _):
+        at = rows_of(c)
+        pltpu.make_async_copy(near_high.at[at, :], phi.at[at, :], high_sem.at[c]).wait()
+        pltpu.make_async_copy(near_low.at[at, :], plo.at[at, :], low_sem.at[c]).wait()
+        return 0
+
+    lax.fori_loop(0, near, end, 0)
+    v0[...] = v0[...] * inverse
+
+    high, low = split(v0[...])
+    stack[:lines] = high
+    stack[lines:] = low
+    acc[...] = jnp.zeros_like(acc)
+
+    def inner_first(c):
+        u = dot(stack[...], phi[rows_of(c), :], NT)
+        uh, ul = split((u[:lines] + u[lines:]) * live[c][0:1])
+        inner[lax.rem(c, 2), :lines] = uh
+        inner[lax.rem(c, 2), lines:] = ul
+
+    def first(c, _):
+        slot = lax.rem(c, 2)
+        held = inner[slot]
+        acc[...] += dot(held, phi[rows_of(c), :], NN)
+        acc[:lines] += dot(held[:lines], plo[rows_of(c), :], NN)
+        inner_first(jnp.minimum(c + 1, chunks - 1))
+        return 0
+
+    inner_first(0)
+    lax.fori_loop(0, chunks, first, 0)
+    image[...] = (acc[:lines] + acc[lines:]) * inverse + ridge_penalty * v0[...]
+    shift0 = estimate(cols, v0, image)
+    q1[...] = v0[...] - shift0 * image[...]
+    stack[:lines] = q1[...].astype(bf16)
+    acc[:lines] = jnp.zeros((lines, acc.shape[1]), f32)
+
+    def inner_second(c):
+        u = dot(stack[:lines], phi[rows_of(c), :], NT) * live[c][0:1]
+        inner[lax.rem(c, 2), :lines] = u.astype(bf16)
+
+    def second(c, _):
+        held = inner[lax.rem(c, 2), :lines]
+        acc[:lines] += dot(held, phi[rows_of(c), :], NN)
+        inner_second(jnp.minimum(c + 1, chunks - 1))
+        return 0
+
+    inner_second(0)
+    lax.fori_loop(0, chunks, second, 0)
+    acc[:lines] = acc[:lines] * inverse + ridge_penalty * q1[...]
+    shift1 = estimate(cols, q1, acc)
+    v0_ref[...] = v0[:cols]
+    q1_ref[...] = q1[:cols]
+    q2_ref[...] = q1[:cols] - shift1 * acc[:cols]
+    stack[:cols] = q2_ref[...].astype(bf16)
+
+    def curve(c, total_sq):
+        u = dot(stack[:cols], phi[rows_of(c), :], NT) * live[c][0:1]
+        return total_sq + u * u
+
+    squares = lax.fori_loop(0, chunks, curve, jnp.zeros((cols, CHUNK), f32))
+    vectors = (v0_ref, q1_ref, q2_ref)
+    images = (image, acc)
+    pairs = [jnp.sum(vectors[i][...] * vectors[j][...]) for i in range(3) for j in range(i, 3)]
+    pairs += [jnp.sum(vectors[i][...] * images[j][:cols]) for j in range(2) for i in range(j, 3)]
+    pairs.append(jnp.sum(squares) / total + ridge_penalty * pairs[5])
+    for i, m in enumerate(pairs):
+        mom_ref[i] = m
+    mom_ref[12] = jnp.sum(shift0)
+    mom_ref[13] = jnp.sum(shift1)
+    mom_ref[14] = total
+    mom_ref[15] = total
+
+
+def finish_kernel(groups, entries, sum_ref, mom_ref, v0_ref, q1_ref, q2_ref, out_ref):
+    f32 = jnp.float32
+
+    def row(ref, i):
+        return jnp.full((1, LANES), ref[i], f32)
+
+    g = {}
+    for n, (i, j) in enumerate(((0, 0), (0, 1), (0, 2), (1, 1), (1, 2), (2, 2))):
+        g[i, j] = g[j, i] = row(sum_ref, n) / entries
+    h = {}
+    for n, (i, j) in enumerate(((0, 0), (1, 0), (2, 0), (1, 1), (2, 1), (2, 2))):
+        h[i, j] = h[j, i] = row(sum_ref, 6 + n) / entries
+    shift0, shift1, total = row(mom_ref, 12), row(mom_ref, 13), row(mom_ref, 14)
+
+    def form(table, r):
+        return sum(r[i] * r[j] * table[i, j] for i in range(3) for j in range(3))
+
+    def step_of(r):
+        return jnp.clip(form(g, r) / (form(h, r) + epsilon), 0.0, 1.0 / ridge_penalty)
+
+    one = jnp.ones((1, LANES), f32)
+    zero = jnp.zeros((1, LANES), f32)
+    r0 = (one, zero, zero)
+    step0 = g[0, 0] / (h[0, 0] + epsilon)
+    ratio = step0 / shift0
+    r1 = (one - ratio, ratio, zero)
+    step1 = step_of(r1)
+    left, right = r1[0] / shift0, r1[1] / shift1
+    r2 = (r1[0] - step1 * left, r1[1] - step1 * (right - left), step1 * right)
+    step2 = step_of(r2)
+    root = jnp.sqrt(total)
+    k = [(root * (step0 * r0[i] + step1 * r1[i] + step2 * r2[i]))[:, :1] for i in range(3)]
+    piece = v0_ref.shape[1] // groups
+    for owner in range(groups):
+        at = slice(owner * piece, (owner + 1) * piece)
+        out_ref[owner] = k[0] * v0_ref[:, at] + k[1] * q1_ref[:, at] + k[2] * q2_ref[:, at]
+
+
+def factor_form(signals, targets, row_counts, feature_weights, phases, spread_ids):
+    _, rows, depth = signals.shape
+    width = feature_weights.shape[1]
+    tgt_width = targets.shape[2]
+    groups = lax.axis_size("asset")
+    epochs = lax.axis_size("epoch")
+    cols = tgt_width // groups
+    mark = cols + SHARED
+    lines = (mark + 1 + SUBLANES - 1) // SUBLANES * SUBLANES
+    piece = width // groups
+    f32, bf16 = jnp.float32, jnp.bfloat16
+    asset = lax.axis_index("asset")
+    epoch = lax.axis_index("epoch")
+
+    def rotate(a, s):
+        return lax.ppermute(a, "asset", [(i, (i + s) % groups) for i in range(groups)])
+
+    def swap(a, bit):
+        return lax.ppermute(a, "epoch", [(e, e ^ bit) for e in range(epochs)])
+
+    x = signals[0]
+    x_own = [x] + [rotate(x, s) for s in range(1, groups)]
+    alive = (jnp.arange(rows) < row_counts[0, 0])[:, None]
+    returns = jnp.where(alive, targets[0], jnp.zeros((), bf16))
+    rest = jnp.concatenate(
+        [returns[:, :SHARED], alive.astype(bf16), jnp.zeros((rows, LANES - mark - 1), bf16)], axis=1
+    )
+    payload = jnp.stack(
+        [
+            jnp.concatenate([returns[:, g * cols : (g + 1) * cols], rest], axis=1)
+            for g in range(groups)
+        ]
+    )
+    y_own = []
+    for s in range(groups):
+        mine = lax.dynamic_index_in_dim(payload, (asset + s) % groups, 0, False)
+        y_own.append(rotate(mine, s) if s else mine)
+    y_own = jnp.concatenate(y_own)
+    held = [(x_own, y_own, 0)]
+    bit = epochs // 2
+    while bit > 1:
+        held = held + [([swap(b, bit) for b in xs], swap(y, bit), o ^ bit) for xs, y, o in held]
+        bit //= 2
+    held = [(jnp.concatenate(xs), y, o) for xs, y, o in held]
+    held = held + [(swap(xs, 1), swap(y, 1), o ^ 1) for xs, y, o in held]
+    near = [h for h in held if h[2] < 2]
+    far = [h for h in held if h[2] >= 2]
+
+    def used(sources):
+        return jnp.stack([((epoch ^ o) <= epoch).astype(jnp.int32) for _, _, o in sources])
+
+    scaled = (feature_weights.astype(f32) * feature_scale(spread_ids)).astype(bf16)
+    offsets = (phases * TURN)[None, :]
+
+    def shape(*dims, dtype=f32):
+        return jax.ShapeDtypeStruct(dims, dtype)
+
+    span = groups * rows
+    limit = len(near) * span
+    high, low, cross, live, info = kernel_call(
+        lambda *refs: near_kernel(len(near), rows, lines, mark, *refs),
+        (
+            shape(limit, width, dtype=bf16),
+            shape(limit, width, dtype=bf16),
+            shape(lines, width),
+            shape(limit // CHUNK, 8, CHUNK),
+            shape(2, dtype=jnp.int32),
+        ),
+        [SCALARS] + [WHOLE] * (2 * len(near) + 2),
+        (REMOTE, REMOTE, WHOLE, WHOLE, SCALARS),
+        [
+            pltpu.VMEM((limit + CHUNK, depth), bf16),
+            pltpu.VMEM((limit + CHUNK, LANES), bf16),
+            pltpu.VMEM((2, CHUNK, width), bf16),
+            pltpu.VMEM((2, CHUNK, width), bf16),
+            pltpu.SemaphoreType.DMA((2,)),
+            pltpu.SemaphoreType.DMA((2,)),
+        ],
+        pl.CostEstimate(flops=10**10, transcendentals=limit * width, bytes_accessed=5 * 10**7),
+    )(used(near), *[a for a, _, _ in near], *[y for _, y, _ in near], scaled, offsets)
+
+    limit = len(far) * span
+    whole = len(held) * span
+    vector = shape(cols, width)
+    v0, q1, q2, moments = kernel_call(
+        lambda *refs: main_kernel(len(far), rows, lines, cols, mark, *refs),
+        (vector, vector, vector, shape(16)),
+        [SCALARS] * 2 + [WHOLE] * (2 * len(far) + 4) + [REMOTE] * 2,
+        (WHOLE, WHOLE, WHOLE, SCALARS),
+        [
+            pltpu.VMEM((limit + CHUNK, depth), bf16),
+            pltpu.VMEM((limit + CHUNK, LANES), bf16),
+            pltpu.VMEM((whole, width), bf16),
+            pltpu.VMEM((whole, width), bf16),
+            pltpu.VMEM((whole // CHUNK, 8, CHUNK), f32),
+            pltpu.VMEM((2 * lines, width), bf16),
+            pltpu.VMEM((2, 2 * lines, CHUNK), bf16),
+            pltpu.VMEM((2 * lines, width), f32),
+            pltpu.VMEM((lines, width), f32),
+            pltpu.VMEM((lines, width), f32),
+            pltpu.VMEM((lines, width), f32),
+            pltpu.SemaphoreType.DMA((len(near) * span // CHUNK,)),
+            pltpu.SemaphoreType.DMA((len(near) * span // CHUNK,)),
+        ],
+    )(
+        used(far), info, *[a for a, _, _ in far], *[y for _, y, _ in far],
+        scaled, offsets, cross, live, high, low,
+    )
+    sums = lax.psum(moments, "asset")
+    coef = kernel_call(
+        lambda *refs: finish_kernel(groups, width * tgt_width, *refs),
+        shape(groups, cols, piece),
+        [SCALARS] * 2 + [WHOLE] * 3,
+        WHOLE,
+        [],
+    )(sums, moments, v0, q1, q2)
+    coef = lax.all_to_all(coef, "asset", 0, 0, tiled=True)
+    return coef.reshape(tgt_width, piece).T[None]
+
+
+def on_device(signals, targets, row_counts, feature_weights, phases, spread_ids):
+    epochs = lax.axis_size("epoch")
+    groups = lax.axis_size("asset")
+    width = feature_weights.shape[1]
+    rows = signals.shape[1]
+    cols = targets.shape[2] // groups
+    fits = (
+        epochs * groups * rows <= 2 * width
+        and epochs & (epochs - 1) == 0
+        and epochs >= 4
+        and rows % CHUNK == 0
+        and width % TILE == 0
+        and cols % 8 == 0
+        and (width // groups) % LANES == 0
+        and cols + SHARED + 8 <= LANES
+    )
+    form = factor_form if fits else gram_form
+    return form(signals, targets, row_counts, feature_weights, phases, spread_ids)
+
+
 def solution(mesh):
     placed = (
         P(("grp", "epoch"), "asset", None),

time: 711 us -> 115 us (0.16)
  waiting for transfers between devices: 550 us -> 9.69 us
  Pallas kernels: 0 us -> 53.2 us
  matrix products: 48 us -> 0 us
  other arithmetic: 37.6 us -> 4.21 us
  starting transfers between devices: 0.39 us -> 20.8 us
  between operations: 18.6 us -> 0.93 us
  blocking collectives: 40.6 us -> 23.3 us
    reduce_scatter x1 -> x0, waiting for transfers between devices: 315 us -> none  [on_device(): lax.psum_scatter(lax.dot_general(features, combined, contract_rows, preci...]
    all_gather x4 -> x0, waiting for transfers between devices: 236 us -> none  [the longest x3 132 us: on_device(): lax.all_gather(residual, 'asset', axis=0, tiled=True)]
    pallas_call x0 -> x3, Pallas kernels: none -> 53.2 us  [the longest x1 35.8 us: factor_form(): kernel_call(lambda *refs: main_kernel(len(far), rows, lines, cols, mark,...]
    dot_general x5 -> x0, matrix products: 48 us -> none  [the longest x3 20.5 us: on_device(): jnp.dot(system, lax.all_gather(residual, 'asset', axis=0, tiled=True), pr...]
    add x6 -> x0, other arithmetic: 29.1 us -> none  [the longest x3 19.7 us: add_pair(): return (earlier[0] + later[0], earlier[1] + later[1])]
    ppermute x0 -> x15, starting transfers between devices: none -> 20.8 us  [the longest x9 13.6 us: swap(): return lax.ppermute(a, 'epoch', [(e, e ^ bit) for e in range(epochs)])]
    psum x3 -> x1, blocking collectives: 25.3 us -> 9.81 us  [factor_form(): sums = lax.psum(moments, 'asset')]
    unnamed x2 -> x0, blocking collectives: 15.4 us -> none
  transfers between devices with their start and end apart: 5 -> 15, of which waited for: 5 -> 4; matrix products, arithmetic and copies ran while one was open for 1% -> 4% of each run, Pallas kernels for 0% -> 13%
where the time goes in v1:
time: 115 us
  Pallas kernels  53.2 us (46%)
  blocking collectives  23.3 us (20%)
  starting transfers between devices  20.8 us (18%)
  waiting for transfers between devices  9.69 us (8%)
  other arithmetic  4.21 us (4%)
  local copies, waits for them, and re-layouts  3.02 us (3%)
    pallas_call x1, Pallas kernels, factor_form(): kernel_call(lambda *refs: main_kernel(len(far), rows, lines, cols, mark,...  35.8 us
    pallas_call x1, Pallas kernels, factor_form(): kernel_call(lambda *refs: near_kernel(len(near), rows, lines, mark, *refs...  15.1 us
    ppermute x9, starting transfers between devices, swap(): return lax.ppermute(a, 'epoch', [(e, e ^ bit) for e in range(epochs)])  13.6 us
    all_to_all x1, blocking collectives, factor_form(): coef = lax.all_to_all(coef, 'asset', 0, 0, tiled=True)  13.5 us
    psum x1, blocking collectives, factor_form(): sums = lax.psum(moments, 'asset')  9.81 us
    ppermute x6, starting transfers between devices, rotate(): lax.ppermute(a, 'asset', [(i, (i + s) % groups) for i in range(groups)])  7.21 us
    ppermute x9, waiting for transfers between devices, swap(): return lax.ppermute(a, 'epoch', [(e, e ^ bit) for e in range(epochs)])  6.76 us
    ppermute x6, waiting for transfers between devices, rotate(): lax.ppermute(a, 'asset', [(i, (i + s) % groups) for i in range(groups)])  2.93 us
  transfers between devices with their start and end apart: 15, of which 4 were waited for; matrix products, arithmetic and copies ran while one was open for 4% of the time, Pallas kernels for 13%

profile of v1, /device:TPU:7, one launch (start us, length us, event | category | flops | bytes accessed | tf_op | source)
XLA Modules:
  0.0 115.2 jit_solution(10992589044353800916)
XLA Ops:
  0.0 0.3 collective-permute-start.8
  0.3 3.3 %collective-permute-start.2 = (bf16[256,256]{1,0:T(8,128)(2,1)}, bf16[256,256]{1,0:T(8,128)(2,1)S(1)}, u32[]{:S(2)}, u32[]{:S(2)}) collective-permute-start(bf16[256,256]{1,0:T(8,128)(2,1)} %bitcast.32), channel_id=1, source_target_pairs={{0,3},{1,0},{2,1},{3,2},{4,7},{5,4},{6,5},{7,6},{8,11},{9,8},{10,9... | collective-permute-start | bytes 393224 | tf_op jit(solution)/shard_map/ppermute | solution.py:413
  3.7 0.5 collective-permute-start
  4.8 1.0 bitcast_select_fusion
  6.1 0.2 maximum_bitcast_fusion
  6.3 2.9 %collective-permute-start.6 = (bf16[256,128]{1,0:T(8,128)(2,1)S(1)}, bf16[256,128]{1,0:T(8,128)(2,1)S(1)}, u32[]{:S(2)}, u32[]{:S(2)}) collective-permute-start(bf16[256,128]{1,0:T(8,128)(2,1)S(1)} %get-tuple-element.24), channel_id=1, source_target_pairs={{0,3},{1,0},{2,1},{3,2},{4,7},{5,4},{6,5},{7,6},{8,11},{9,8},{10,9... | collective-permute-start | bytes 196616 | tf_op jit(solution)/shard_map/ppermute | solution.py:413
  9.2 0.6 broadcast_multiply_fusion
  9.8 1.2 %multiply_convert_fusion.refs_5_.refs_6_ = bf16[256,2048]{1,0:T(8,128)(2,1)} fusion(bf16[256,2048]{1,0:T(8,128)(2,1)S(1)} %copy-done, f32[2048]{0:T(1024)S(1)} %add_multiply_fusion), kind=kLoop, calls=%fused_computation | loop fusion | flops 1572864 | bytes 2105344 | tf_op jit(solution)/shard_map/convert_element_type | solution.py:449
  11.0 0.6 add_convert_fusion.refs_0_
  11.6 0.6 add_convert_fusion.1.refs_0_
  12.1 0.6 collective-permute-start.5
  12.7 2.0 %collective-permute-done.1 = bf16[256,256]{1,0:T(8,128)(2,1)S(1)} collective-permute-done((bf16[256,256]{1,0:T(8,128)(2,1)}, bf16[256,256]{1,0:T(8,128)(2,1)S(1)}, u32[]{:S(2)}, u32[]{:S(2)}) %collective-permute-start.1) | collective-permute-done | bytes 131104 | tf_op jit(solution)/shard_map/ppermute | solution.py:413
  14.8 2.8 %collective-permute-start.3 = (bf16[1024,256]{1,0:T(8,128)(2,1)S(1)}, bf16[1024,256]{1,0:T(8,128)(2,1)S(1)}, u32[]{:S(2)}, u32[]{:S(2)}) collective-permute-start(bf16[1024,256]{1,0:T(8,128)(2,1)S(1)} %pad_maximum_fusion.refs_1_), channel_id=1, source_target_pairs={{0,4},{4,0},{8,12},{12,8},{1,5},{5,1},{9,13},{13,9},{2,6},{6,2},{1... | collective-permute-start | bytes 1572872 | tf_op jit(solution)/shard_map/ppermute | solution.py:416
  17.6 1.2 %collective-permute-start.9 = (bf16[256,256]{1,0:T(8,128)(2,1)S(1)}, bf16[256,256]{1,0:T(8,128)(2,1)S(1)}, u32[]{:S(2)}, u32[]{:S(2)}) collective-permute-start(bf16[256,256]{1,0:T(8,128)(2,1)S(1)} %collective-permute-done), channel_id=1, source_target_pairs={{0,8},{4,12},{8,0},{12,4},{1,9},{5,13},{9,1},{13,5},{2,10},{6,14},... | collective-permute-start | bytes 393224 | tf_op jit(solution)/shard_map/ppermute | solution.py:416
  18.8 0.9 collective-permute-done.4
  19.8 1.3 %collective-permute-start.13 = (bf16[1024,128]{1,0:T(8,128)(2,1)S(1)}, bf16[1024,128]{1,0:T(8,128)(2,1)S(1)}, u32[]{:S(2)}, u32[]{:S(2)}) collective-permute-start(bf16[1024,128]{1,0:T(8,128)(2,1)S(1)} %pad_maximum_fusion.2.refs_3_), channel_id=1, source_target_pairs={{0,8},{4,12},{8,0},{12,4},{1,9},{5,13},{9,1},{13,5},{2,10},{6,14},... | collective-permute-start | bytes 786440 | tf_op jit(solution)/shard_map/ppermute | solution.py:416
  21.0 4.1 %collective-permute-start.7 = (bf16[1024,128]{1,0:T(8,128)(2,1)S(1)}, bf16[1024,128]{1,0:T(8,128)(2,1)S(1)}, u32[]{:S(2)}, u32[]{:S(2)}) collective-permute-start(bf16[1024,128]{1,0:T(8,128)(2,1)S(1)} %pad_maximum_fusion.2.refs_3_), channel_id=1, source_target_pairs={{0,4},{4,0},{8,12},{12,8},{1,5},{5,1},{9,13},{13,9},{2,6},{6,2},{1... | collective-permute-start | bytes 786440 | tf_op jit(solution)/shard_map/ppermute | solution.py:416
  25.1 0.3 collective-permute-start.10
  25.4 1.3 %collective-permute-start.11 = (bf16[256,256]{1,0:T(8,128)(2,1)S(1)}, bf16[256,256]{1,0:T(8,128)(2,1)S(1)}, u32[]{:S(2)}, u32[]{:S(2)}) collective-permute-start(bf16[256,256]{1,0:T(8,128)(2,1)S(1)} %collective-permute-done.2), channel_id=1, source_target_pairs={{0,8},{4,12},{8,0},{12,4},{1,9},{5,13},{9,1},{13,5},{2,10},{6,14},... | collective-permute-start | bytes 393224 | tf_op jit(solution)/shard_map/ppermute | solution.py:416
  26.7 3.9 %collective-permute-done.10 = bf16[256,256]{1,0:T(8,128)(2,1)S(1)} collective-permute-done((bf16[256,256]{1,0:T(8,128)(2,1)S(1)}, bf16[256,256]{1,0:T(8,128)(2,1)S(1)}, u32[]{:S(2)}, u32[]{:S(2)}) %collective-permute-start.10) | collective-permute-done | bytes 131104 | tf_op jit(solution)/shard_map/ppermute | solution.py:416
  30.7 2.8 %collective-permute-done.11 = bf16[256,256]{1,0:T(8,128)(2,1)S(1)} collective-permute-done((bf16[256,256]{1,0:T(8,128)(2,1)S(1)}, bf16[256,256]{1,0:T(8,128)(2,1)S(1)}, u32[]{:S(2)}, u32[]{:S(2)}) %collective-permute-start.11) | collective-permute-done | bytes 131104 | tf_op jit(solution)/shard_map/ppermute | solution.py:416
  33.5 2.2 %collective-permute-start.12 = (bf16[1024,256]{1,0:T(8,128)(2,1)S(1)}, bf16[1024,256]{1,0:T(8,128)(2,1)S(1)}, u32[]{:S(2)}, u32[]{:S(2)}) collective-permute-start(bf16[1024,256]{1,0:T(8,128)(2,1)S(1)} %constant_dynamic-update-slice_fusion.refs_2_), channel_id=1, source_target_pairs={{0,4},{4,0},{8,12},{12,8},{1,5},{5,1},{9,13},{13,9},{2,6},{6,2},{1... | collective-permute-start | bytes 1572872 | tf_op jit(solution)/shard_map/ppermute | solution.py:416
  35.9 0.7 copy-done.11
  36.5 0.2 copy-done.10
  36.7 15.1 %shard_map.64 = (bf16[2048,2048]{1,0:T(8,128)(2,1)}, bf16[2048,2048]{1,0:T(8,128)(2,1)}, f32[80,2048]{1,0:T(8,128)}, f32[8,8,256]{2,1,0:T(8,128)}, s32[2]{0:T(128)}) custom-call(s32[2]{0:T(128)} %add_convert_fusion.1.refs_0_, bf16[1024,256]{1,0:T(8,128)(2,1)} %copy-done.3, bf16[1024,256]{1,0:T(8,128)(2,1)} %copy-done.10, bf16[1024,128]{1,0:T(8,128)(2,1)} %copy-done.6, ...), custom_call_target="tpu_custom_call" | custom-call | flops 10000000000 | bytes 50000000 | tf_op jit(solution)/shard_map/pallas_call | solution.py:457
  51.9 0.7 copy-done.5
  52.6 0.2 copy-done.2
  52.7 35.8 %shard_map.65 = (f32[64,2048]{1,0:T(8,128)}, f32[64,2048]{1,0:T(8,128)}, f32[64,2048]{1,0:T(8,128)}, f32[16]{0:T(128)}) custom-call(s32[2]{0:T(128)} %add_convert_fusion.refs_0_, s32[2]{0:T(128)} %get-tuple-element.14.refs_1_, bf16[1024,256]{1,0:T(8,128)(2,1)} %copy-done.1, bf16[1024,256]{1,0:T(8,128)(2,1)} %copy-done.2, bf16[1024,128]{1,0:T(8,128)(2,1)} %copy-done.4, ...), custom_call_target="tpu_custom_call" | custom-call | tf_op jit(solution)/shard_map/pallas_call | solution.py:482
  88.5 9.8 %psum.7.refs_0_ = f32[16]{0:T(128)} all-reduce(f32[16]{0:T(128)} %get-tuple-element.19.refs_1_), channel_id=1, replica_groups=mesh['grp'=2,'epoch'=4,'asset'=4] {'asset'}, use_global_device_ids=true, to_apply=%region_0.1 | all-reduce | flops 16 | bytes 128 | tf_op jit(solution)/shard_map/psum | solution.py:506
  98.4 2.3 %shard_map.66 = f32[4,64,512]{2,1,0:T(8,128)} custom-call(f32[16]{0:T(128)} %psum.7.refs_0_, f32[16]{0:T(128)} %get-tuple-element.19.refs_1_, f32[64,2048]{1,0:T(8,128)} %get-tuple-element.20.refs_2_, f32[64,2048]{1,0:T(8,128)} %get-tuple-element.21.refs_3_, f32[64,2048]{1,0:T(8,128)} %get-tuple-element.22.refs_4_), custom_call_target="tpu_custom_call" | custom-call | tf_op jit(solution)/shard_map/pallas_call | solution.py:507
  100.7 13.5 %all_to_all.5 = f32[4,64,512]{2,1,0:T(8,128)S(1)} all-to-all(f32[4,64,512]{2,1,0:T(8,128)} %shard_map.66), channel_id=1, replica_groups=mesh['grp'=2,'epoch'=4,'asset'=4] {'asset'}, dimensions={0} | all-to-all | bytes 1048576 | tf_op jit(solution)/shard_map/all_to_all | solution.py:514
  114.2 1.0 copy.7
  (49 shorter events, 0.6 us)
Async XLA Ops:
  0.0 9.2 %copy-start.8 = (f32[2048]{0:T(1024)S(1)}, f32[2048]{0:T(1024)}, u32[]{:S(2)}) copy-start(f32[2048]{0:T(1024)} %param.10) | copy-start | bytes 24580
  0.0 9.8 %copy-start.9 = (s32[2048]{0:T(1024)S(1)}, s32[2048]{0:T(1024)}, u32[]{:S(2)}) copy-start(s32[2048]{0:T(1024)} %param.11) | copy-start | bytes 24580
  0.0 9.8 %copy-start = (bf16[256,2048]{1,0:T(8,128)(2,1)S(1)}, bf16[256,2048]{1,0:T(8,128)(2,1)}, u32[]{:S(2)}) copy-start(bf16[256,2048]{1,0:T(8,128)(2,1)} %param.9) | copy-start | bytes 3145732
  0.0 25.1 %collective-permute-start.8 = (bf16[256,256]{1,0:T(8,128)(2,1)}, bf16[256,256]{1,0:T(8,128)(2,1)S(1)}, u32[]{:S(2)}, u32[]{:S(2)}) collective-permute-start(bf16[256,256]{1,0:T(8,128)(2,1)} %bitcast.31), channel_id=1, source_target_pairs={{0,8},{4,12},{8,0},{12,4},{1,9},{5,13},{9,1},{13,5},{2,10},{6,14},... | collective-permute-start | bytes 393224 | tf_op jit(solution)/shard_map/ppermute | solution.py:416
  0.3 11.8 %collective-permute-start.2 = (bf16[256,256]{1,0:T(8,128)(2,1)}, bf16[256,256]{1,0:T(8,128)(2,1)S(1)}, u32[]{:S(2)}, u32[]{:S(2)}) collective-permute-start(bf16[256,256]{1,0:T(8,128)(2,1)} %bitcast.32), channel_id=1, source_target_pairs={{0,3},{1,0},{2,1},{3,2},{4,7},{5,4},{6,5},{7,6},{8,11},{9,8},{10,9... | collective-permute-start | bytes 393224 | tf_op jit(solution)/shard_map/ppermute | solution.py:413
  3.7 11.1 %collective-permute-start.1 = (bf16[256,256]{1,0:T(8,128)(2,1)}, bf16[256,256]{1,0:T(8,128)(2,1)S(1)}, u32[]{:S(2)}, u32[]{:S(2)}) collective-permute-start(bf16[256,256]{1,0:T(8,128)(2,1)} %bitcast.33), channel_id=1, source_target_pairs={{0,2},{1,3},{2,0},{3,1},{4,6},{5,7},{6,4},{7,5},{8,10},{9,11},{10,... | collective-permute-start | bytes 393224 | tf_op jit(solution)/shard_map/ppermute | solution.py:413
  3.7 11.1 %collective-permute-start = (bf16[256,256]{1,0:T(8,128)(2,1)}, bf16[256,256]{1,0:T(8,128)(2,1)S(1)}, u32[]{:S(2)}, u32[]{:S(2)}) collective-permute-start(bf16[256,256]{1,0:T(8,128)(2,1)} %bitcast.34), channel_id=1, source_target_pairs={{0,1},{1,2},{2,3},{3,0},{4,5},{5,6},{6,7},{7,4},{8,9},{9,10},{10,1... | collective-permute-start | bytes 393224 | tf_op jit(solution)/shard_map/ppermute | solution.py:413
  5.9 8.8 %copy-start.7 = (bf16[1,256,256]{2,1,0:T(8,128)(2,1)S(1)}, bf16[1,256,256]{2,1,0:T(8,128)(2,1)}, u32[]{:S(2)}) copy-start(bf16[1,256,256]{2,1,0:T(8,128)(2,1)} %param.6) | copy-start | bytes 393220
  6.3 11.3 %collective-permute-start.6 = (bf16[256,128]{1,0:T(8,128)(2,1)S(1)}, bf16[256,128]{1,0:T(8,128)(2,1)S(1)}, u32[]{:S(2)}, u32[]{:S(2)}) collective-permute-start(bf16[256,128]{1,0:T(8,128)(2,1)S(1)} %get-tuple-element.24), channel_id=1, source_target_pairs={{0,3},{1,0},{2,1},{3,2},{4,7},{5,4},{6,5},{7,6},{8,11},{9,8},{10,9... | collective-permute-start | bytes 196616 | tf_op jit(solution)/shard_map/ppermute | solution.py:413
  12.1 6.7 %collective-permute-start.5 = (bf16[256,128]{1,0:T(8,128)(2,1)S(1)}, bf16[256,128]{1,0:T(8,128)(2,1)S(1)}, u32[]{:S(2)}, u32[]{:S(2)}) collective-permute-start(bf16[256,128]{1,0:T(8,128)(2,1)S(1)} %get-tuple-element.25), channel_id=1, source_target_pairs={{0,2},{1,3},{2,0},{3,1},{4,6},{5,7},{6,4},{7,5},{8,10},{9,11},{10,... | collective-permute-start | bytes 196616 | tf_op jit(solution)/shard_map/ppermute | solution.py:413
  14.7 5.0 %collective-permute-start.4 = (bf16[256,128]{1,0:T(8,128)(2,1)S(1)}, bf16[256,128]{1,0:T(8,128)(2,1)S(1)}, u32[]{:S(2)}, u32[]{:S(2)}) collective-permute-start(bf16[256,128]{1,0:T(8,128)(2,1)S(1)} %get-tuple-element.26), channel_id=1, source_target_pairs={{0,1},{1,2},{2,3},{3,0},{4,5},{5,6},{6,7},{7,4},{8,9},{9,10},{10,1... | collective-permute-start | bytes 196616 | tf_op jit(solution)/shard_map/ppermute | solution.py:413
  14.8 21.1 %copy-start.3 = (bf16[1024,256]{1,0:T(8,128)(2,1)}, bf16[1024,256]{1,0:T(8,128)(2,1)S(1)}, u32[]{:S(2)}) copy-start(bf16[1024,256]{1,0:T(8,128)(2,1)S(1)} %pad_maximum_fusion.refs_1_) | copy-start | bytes 1572868
  14.8 21.0 %collective-permute-start.3 = (bf16[1024,256]{1,0:T(8,128)(2,1)S(1)}, bf16[1024,256]{1,0:T(8,128)(2,1)S(1)}, u32[]{:S(2)}, u32[]{:S(2)}) collective-permute-start(bf16[1024,256]{1,0:T(8,128)(2,1)S(1)} %pad_maximum_fusion.refs_1_), channel_id=1, source_target_pairs={{0,4},{4,0},{8,12},{12,8},{1,5},{5,1},{9,13},{13,9},{2,6},{6,2},{1... | collective-permute-start | bytes 1572872 | tf_op jit(solution)/shard_map/ppermute | solution.py:416
  17.6 7.8 %collective-permute-start.9 = (bf16[256,256]{1,0:T(8,128)(2,1)S(1)}, bf16[256,256]{1,0:T(8,128)(2,1)S(1)}, u32[]{:S(2)}, u32[]{:S(2)}) collective-permute-start(bf16[256,256]{1,0:T(8,128)(2,1)S(1)} %collective-permute-done), channel_id=1, source_target_pairs={{0,8},{4,12},{8,0},{12,4},{1,9},{5,13},{9,1},{13,5},{2,10},{6,14},... | collective-permute-start | bytes 393224 | tf_op jit(solution)/shard_map/ppermute | solution.py:416
  19.7 16.1 %copy-start.6 = (bf16[1024,128]{1,0:T(8,128)(2,1)}, bf16[1024,128]{1,0:T(8,128)(2,1)S(1)}, u32[]{:S(2)}) copy-start(bf16[1024,128]{1,0:T(8,128)(2,1)S(1)} %pad_maximum_fusion.2.refs_3_) | copy-start | bytes 786436
  19.8 16.0 %collective-permute-start.13 = (bf16[1024,128]{1,0:T(8,128)(2,1)S(1)}, bf16[1024,128]{1,0:T(8,128)(2,1)S(1)}, u32[]{:S(2)}, u32[]{:S(2)}) collective-permute-start(bf16[1024,128]{1,0:T(8,128)(2,1)S(1)} %pad_maximum_fusion.2.refs_3_), channel_id=1, source_target_pairs={{0,8},{4,12},{8,0},{12,4},{1,9},{5,13},{9,1},{13,5},{2,10},{6,14},... | collective-permute-start | bytes 786440 | tf_op jit(solution)/shard_map/ppermute | solution.py:416
  21.0 14.8 %collective-permute-start.7 = (bf16[1024,128]{1,0:T(8,128)(2,1)S(1)}, bf16[1024,128]{1,0:T(8,128)(2,1)S(1)}, u32[]{:S(2)}, u32[]{:S(2)}) collective-permute-start(bf16[1024,128]{1,0:T(8,128)(2,1)S(1)} %pad_maximum_fusion.2.refs_3_), channel_id=1, source_target_pairs={{0,4},{4,0},{8,12},{12,8},{1,5},{5,1},{9,13},{13,9},{2,6},{6,2},{1... | collective-permute-start | bytes 786440 | tf_op jit(solution)/shard_map/ppermute | solution.py:416
  25.1 5.5 %collective-permute-start.10 = (bf16[256,256]{1,0:T(8,128)(2,1)S(1)}, bf16[256,256]{1,0:T(8,128)(2,1)S(1)}, u32[]{:S(2)}, u32[]{:S(2)}) collective-permute-start(bf16[256,256]{1,0:T(8,128)(2,1)S(1)} %collective-permute-done.1), channel_id=1, source_target_pairs={{0,8},{4,12},{8,0},{12,4},{1,9},{5,13},{9,1},{13,5},{2,10},{6,14},... | collective-permute-start | bytes 393224 | tf_op jit(solution)/shard_map/ppermute | solution.py:416
  25.4 8.0 %collective-permute-start.11 = (bf16[256,256]{1,0:T(8,128)(2,1)S(1)}, bf16[256,256]{1,0:T(8,128)(2,1)S(1)}, u32[]{:S(2)}, u32[]{:S(2)}) collective-permute-start(bf16[256,256]{1,0:T(8,128)(2,1)S(1)} %collective-permute-done.2), channel_id=1, source_target_pairs={{0,8},{4,12},{8,0},{12,4},{1,9},{5,13},{9,1},{13,5},{2,10},{6,14},... | collective-permute-start | bytes 393224 | tf_op jit(solution)/shard_map/ppermute | solution.py:416
  33.5 18.4 %copy-start.1 = (bf16[1024,256]{1,0:T(8,128)(2,1)}, bf16[1024,256]{1,0:T(8,128)(2,1)S(1)}, u32[]{:S(2)}) copy-start(bf16[1024,256]{1,0:T(8,128)(2,1)S(1)} %constant_dynamic-update-slice_fusion.refs_2_) | copy-start | bytes 1572868
  33.5 18.4 %collective-permute-start.12 = (bf16[1024,256]{1,0:T(8,128)(2,1)S(1)}, bf16[1024,256]{1,0:T(8,128)(2,1)S(1)}, u32[]{:S(2)}, u32[]{:S(2)}) collective-permute-start(bf16[1024,256]{1,0:T(8,128)(2,1)S(1)} %constant_dynamic-update-slice_fusion.refs_2_), channel_id=1, source_target_pairs={{0,4},{4,0},{8,12},{12,8},{1,5},{5,1},{9,13},{13,9},{2,6},{6,2},{1... | collective-permute-start | bytes 1572872 | tf_op jit(solution)/shard_map/ppermute | solution.py:416
  35.7 16.1 %copy-start.4 = (bf16[1024,128]{1,0:T(8,128)(2,1)}, bf16[1024,128]{1,0:T(8,128)(2,1)S(1)}, u32[]{:S(2)}) copy-start(bf16[1024,128]{1,0:T(8,128)(2,1)S(1)} %collective-permute-done.13.refs_4_) | copy-start | bytes 786436
  35.7 16.1 %collective-permute-start.14 = (bf16[1024,128]{1,0:T(8,128)(2,1)S(1)}, bf16[1024,128]{1,0:T(8,128)(2,1)S(1)}, u32[]{:S(2)}, u32[]{:S(2)}) collective-permute-start(bf16[1024,128]{1,0:T(8,128)(2,1)S(1)} %collective-permute-done.13.refs_4_), channel_id=1, source_target_pairs={{0,4},{4,0},{8,12},{12,8},{1,5},{5,1},{9,13},{13,9},{2,6},{6,2},{1... | collective-permute-start | bytes 786440 | tf_op jit(solution)/shard_map/ppermute | solution.py:416
  35.8 0.7 copy-start.11
  35.8 0.9 copy-start.10
  51.9 0.7 copy-start.5
  51.9 0.9 copy-start.2

commit v2 on v1

--- a/solution.py
+++ b/solution.py
@@ -5,6 +5,7 @@
 from jax.experimental.pallas import tpu as pltpu
 from jax.sharding import PartitionSpec as P
 
+
 ITERS = 3
 
 
@@ -12,6 +13,7 @@
 epsilon = 1e-06
 
 CHUNK = 256
+GROUP = 4
 TILE = 256
 PACK = 16
 SHARED = 8
@@ -103,7 +105,7 @@
     ).astype(jnp.float32)
     residual = cumulative[:, width:] / row_total
     coef = jnp.zeros((block_size, tgt_width), jnp.float32)
-    for iteration in range(ITERS):
+    for _ in range(ITERS):
         image = jnp.zeros((block_size, tgt_width), jnp.float32) + jnp.dot(
             system,
             lax.all_gather(residual, "asset", axis=0, tiled=True),
@@ -192,6 +194,19 @@
         cross_ref[:, js] += dot(returns, high, NN) + dot(returns, low, NN)
 
 
+def in_pairs(chunks, one):
+    def pair(p, _):
+        one(2 * p, 0)
+        one(2 * p + 1, 1)
+        return 0
+
+    lax.fori_loop(0, chunks // 2, pair, 0)
+
+    @pl.when(lax.rem(chunks, 2) == 1)
+    def _():
+        one(chunks - 1, 0)
+
+
 def near_kernel(sources, rows, lines, mark, use_ref, *refs):
     x_refs, y_refs = refs[:sources], refs[sources : 2 * sources]
     w_ref, ph_ref, high_hbm, low_hbm, cross_ref, live_ref, info_ref = refs[2 * sources : 2 * sources + 7]
@@ -208,9 +223,7 @@
             pltpu.make_async_copy(low_buf.at[slot], low_hbm.at[rows_of(c), :], low_sem.at[slot]),
         )
 
-    def one(c, _):
-        slot = lax.rem(c, 2)
-
+    def one(c, slot):
         @pl.when(c >= 2)
         def _():
             for copy in send(c - 2, slot):
@@ -226,9 +239,8 @@
         featurize_chunk(x_buf[rows_of(c), :], turned, lines, w_ref, ph_ref, cross_ref, put)
         for copy in send(c, slot):
             copy.start()
-        return 0
-
-    lax.fori_loop(0, chunks, one, 0)
+
+    in_pairs(chunks, one)
     for back in (2, 1):
 
         @pl.when(chunks >= back)
@@ -280,9 +292,17 @@
             plo[at, js] = low
 
         featurize_chunk(x_buf[rows_of(c), :], turned, lines, w_ref, ph_ref, v0, put)
+
+    in_pairs(far, featurize)
+    spans = (chunks + GROUP - 1) // GROUP
+
+    def blank(c, _):
+        phi[rows_of(c), :] = jnp.zeros((CHUNK, phi.shape[1]), bf16)
+        plo[rows_of(c), :] = jnp.zeros((CHUNK, phi.shape[1]), bf16)
+        live[c] = jnp.zeros(live.shape[1:], f32)
         return 0
 
-    lax.fori_loop(0, far, featurize, 0)
+    lax.fori_loop(chunks, spans * GROUP, blank, 0)
 
     def end(c, _):
         at = rows_of(c)
@@ -293,45 +313,47 @@
     lax.fori_loop(0, near, end, 0)
     v0[...] = v0[...] * inverse
 
+    def span_of(p):
+        return pl.ds(pl.multiple_of(p * GROUP * CHUNK, GROUP * CHUNK), GROUP * CHUNK)
+
+    def inner_of(p, part, lefts):
+        half = GROUP // 2
+        first = pl.multiple_of((p * 2 + part) * half * CHUNK, half * CHUNK)
+        mask = jnp.concatenate([live[p * GROUP + part * half + c][0:1] for c in range(half)], axis=1)
+        return dot(lefts, phi[pl.ds(first, half * CHUNK), :], NT), mask
+
     high, low = split(v0[...])
     stack[:lines] = high
     stack[lines:] = low
     acc[...] = jnp.zeros_like(acc)
 
-    def inner_first(c):
-        u = dot(stack[...], phi[rows_of(c), :], NT)
-        uh, ul = split((u[:lines] + u[lines:]) * live[c][0:1])
-        inner[lax.rem(c, 2), :lines] = uh
-        inner[lax.rem(c, 2), lines:] = ul
-
-    def first(c, _):
-        slot = lax.rem(c, 2)
-        held = inner[slot]
-        acc[...] += dot(held, phi[rows_of(c), :], NN)
-        acc[:lines] += dot(held[:lines], plo[rows_of(c), :], NN)
-        inner_first(jnp.minimum(c + 1, chunks - 1))
+    def first(p, _):
+        for part in range(2):
+            u, mask = inner_of(p, part, stack[...])
+            uh, ul = split((u[:lines] + u[lines:]) * mask)
+            at = slice(part * GROUP // 2 * CHUNK, (part + 1) * GROUP // 2 * CHUNK)
+            inner[:lines, at] = uh
+            inner[lines:, at] = ul
+        acc[...] += dot(inner[...], phi[span_of(p), :], NN)
+        acc[:lines] += dot(inner[:lines], plo[span_of(p), :], NN)
         return 0
 
-    inner_first(0)
-    lax.fori_loop(0, chunks, first, 0)
+    lax.fori_loop(0, spans, first, 0)
     image[...] = (acc[:lines] + acc[lines:]) * inverse + ridge_penalty * v0[...]
     shift0 = estimate(cols, v0, image)
     q1[...] = v0[...] - shift0 * image[...]
     stack[:lines] = q1[...].astype(bf16)
     acc[:lines] = jnp.zeros((lines, acc.shape[1]), f32)
 
-    def inner_second(c):
-        u = dot(stack[:lines], phi[rows_of(c), :], NT) * live[c][0:1]
-        inner[lax.rem(c, 2), :lines] = u.astype(bf16)
-
-    def second(c, _):
-        held = inner[lax.rem(c, 2), :lines]
-        acc[:lines] += dot(held, phi[rows_of(c), :], NN)
-        inner_second(jnp.minimum(c + 1, chunks - 1))
+    def second(p, _):
+        for part in range(2):
+            u, mask = inner_of(p, part, stack[:lines])
+            at = slice(part * GROUP // 2 * CHUNK, (part + 1) * GROUP // 2 * CHUNK)
+            inner[:lines, at] = (u * mask).astype(bf16)
+        acc[:lines] += dot(inner[:lines], phi[span_of(p), :], NN)
         return 0
 
-    inner_second(0)
-    lax.fori_loop(0, chunks, second, 0)
+    lax.fori_loop(0, spans, second, 0)
     acc[:lines] = acc[:lines] * inverse + ridge_penalty * q1[...]
     shift1 = estimate(cols, q1, acc)
     v0_ref[...] = v0[:cols]
@@ -339,11 +361,13 @@
     q2_ref[...] = q1[:cols] - shift1 * acc[:cols]
     stack[:cols] = q2_ref[...].astype(bf16)
 
-    def curve(c, total_sq):
-        u = dot(stack[:cols], phi[rows_of(c), :], NT) * live[c][0:1]
-        return total_sq + u * u
-
-    squares = lax.fori_loop(0, chunks, curve, jnp.zeros((cols, CHUNK), f32))
+    def curve(p, total_sq):
+        for part in range(2):
+            u, mask = inner_of(p, part, stack[:cols])
+            total_sq = total_sq + jnp.square(u * mask)
+        return total_sq
+
+    squares = lax.fori_loop(0, spans, curve, jnp.zeros((cols, GROUP // 2 * CHUNK), f32))
     vectors = (v0_ref, q1_ref, q2_ref)
     images = (image, acc)
     pairs = [jnp.sum(vectors[i][...] * vectors[j][...]) for i in range(3) for j in range(i, 3)]
@@ -357,19 +381,25 @@
     mom_ref[15] = total
 
 
-def finish_kernel(groups, entries, sum_ref, mom_ref, v0_ref, q1_ref, q2_ref, out_ref):
+def finish_kernel(groups, entries, *refs):
+    share_refs = refs[:groups]
+    mom_ref = share_refs[0]
+    v0_ref, q1_ref, q2_ref, out_ref = refs[groups:]
     f32 = jnp.float32
 
-    def row(ref, i):
-        return jnp.full((1, LANES), ref[i], f32)
+    def local(i):
+        return jnp.full((1, LANES), mom_ref[i], f32)
+
+    def mean(i):
+        return jnp.full((1, LANES), sum(ref[i] for ref in share_refs), f32) / entries
 
     g = {}
     for n, (i, j) in enumerate(((0, 0), (0, 1), (0, 2), (1, 1), (1, 2), (2, 2))):
-        g[i, j] = g[j, i] = row(sum_ref, n) / entries
+        g[i, j] = g[j, i] = mean(n)
     h = {}
     for n, (i, j) in enumerate(((0, 0), (1, 0), (2, 0), (1, 1), (2, 1), (2, 2))):
-        h[i, j] = h[j, i] = row(sum_ref, 6 + n) / entries
-    shift0, shift1, total = row(mom_ref, 12), row(mom_ref, 13), row(mom_ref, 14)
+        h[i, j] = h[j, i] = mean(6 + n)
+    shift0, shift1, total = local(12), local(13), local(14)
 
     def form(table, r):
         return sum(r[i] * r[j] * table[i, j] for i in range(3) for j in range(3))
@@ -436,12 +466,15 @@
     held = [(x_own, y_own, 0)]
     bit = epochs // 2
     while bit > 1:
-        held = held + [([swap(b, bit) for b in xs], swap(y, bit), o ^ bit) for xs, y, o in held]
+        more = []
+        for xs, y, o in held:
+            more.append(([swap(b, bit) for b in xs], swap(y, bit), o ^ bit))
+        held = held + more
         bit //= 2
     held = [(jnp.concatenate(xs), y, o) for xs, y, o in held]
     held = held + [(swap(xs, 1), swap(y, 1), o ^ 1) for xs, y, o in held]
-    near = [h for h in held if h[2] < 2]
-    far = [h for h in held if h[2] >= 2]
+    near = [h for h in held if h[2] == 0]
+    far = [h for h in held if h[2] != 0]
 
     def used(sources):
         return jnp.stack([((epoch ^ o) <= epoch).astype(jnp.int32) for _, _, o in sources])
@@ -491,7 +524,7 @@
             pltpu.VMEM((whole, width), bf16),
             pltpu.VMEM((whole // CHUNK, 8, CHUNK), f32),
             pltpu.VMEM((2 * lines, width), bf16),
-            pltpu.VMEM((2, 2 * lines, CHUNK), bf16),
+            pltpu.VMEM((2 * lines, GROUP * CHUNK), bf16),
             pltpu.VMEM((2 * lines, width), f32),
             pltpu.VMEM((lines, width), f32),
             pltpu.VMEM((lines, width), f32),
@@ -503,14 +536,14 @@
         used(far), info, *[a for a, _, _ in far], *[y for _, y, _ in far],
         scaled, offsets, cross, live, high, low,
     )
-    sums = lax.psum(moments, "asset")
+    shares = [rotate(moments, s) if s else moments for s in range(groups)]
     coef = kernel_call(
         lambda *refs: finish_kernel(groups, width * tgt_width, *refs),
         shape(groups, cols, piece),
-        [SCALARS] * 2 + [WHOLE] * 3,
+        [SCALARS] * groups + [WHOLE] * 3,
         WHOLE,
         [],
-    )(sums, moments, v0, q1, q2)
+    )(*shares, v0, q1, q2)
     coef = lax.all_to_all(coef, "asset", 0, 0, tiled=True)
     return coef.reshape(tgt_width, piece).T[None]
 
@@ -526,6 +559,7 @@
         and epochs & (epochs - 1) == 0
         and epochs >= 4
         and rows % CHUNK == 0
+        and epochs * groups * rows % (GROUP * CHUNK) == 0
         and width % TILE == 0
         and cols % 8 == 0
         and (width // groups) % LANES == 0

time: 115 us -> 124 us (1.078)
  the two profiles are of different devices: /device:TPU:7 before, /device:TPU:3 now
where the time goes in v2:
time: 124 us; the launch traced here: 123 us
  Pallas kernels  59.9 us (48%)
  starting transfers between devices  23.8 us (19%)
  waiting for transfers between devices  19.6 us (16%)
  blocking collectives  12.6 us (10%)
  other arithmetic  3.77 us (3%)
  local copies, waits for them, and re-layouts  2.9 us (2%)
    pallas_call x1, Pallas kernels, factor_form(): kernel_call(lambda *refs: main_kernel(len(far), rows, lines, cols, mark,...  46.6 us
    ppermute x9, starting transfers between devices, rotate(): lax.ppermute(a, 'asset', [(i, (i + s) % groups) for i in range(groups)])  15.6 us
    ppermute x9, waiting for transfers between devices, swap(): return lax.ppermute(a, 'epoch', [(e, e ^ bit) for e in range(epochs)])  12.7 us
    all_to_all x1, blocking collectives, factor_form(): coef = lax.all_to_all(coef, 'asset', 0, 0, tiled=True)  12.6 us
    pallas_call x1, Pallas kernels, factor_form(): kernel_call(lambda *refs: near_kernel(len(near), rows, lines, mark, *refs...  11 us
    ppermute x9, starting transfers between devices, swap(): return lax.ppermute(a, 'epoch', [(e, e ^ bit) for e in range(epochs)])  8.21 us
    ppermute x9, waiting for transfers between devices, rotate(): lax.ppermute(a, 'asset', [(i, (i + s) % groups) for i in range(groups)])  6.84 us
  transfers between devices with their start and end apart: 18, of which 8 were waited for; matrix products, arithmetic and copies ran while one was open for 3% of the time, Pallas kernels for 9%

profile of v2, /device:TPU:3, one launch (start us, length us, event | category | flops | bytes accessed | tf_op | source)
XLA Modules:
  0.0 123.5 jit_solution(7332628184358887093)
XLA Ops:
  0.0 3.3 %collective-permute-start.2 = (bf16[256,256]{1,0:T(8,128)(2,1)}, bf16[256,256]{1,0:T(8,128)(2,1)S(1)}, u32[]{:S(2)}, u32[]{:S(2)}) collective-permute-start(bf16[256,256]{1,0:T(8,128)(2,1)} %bitcast.31), channel_id=1, source_target_pairs={{0,3},{1,0},{2,1},{3,2},{4,7},{5,4},{6,5},{7,6},{8,11},{9,8},{10,9... | collective-permute-start | bytes 393224 | tf_op jit(solution)/shard_map/ppermute | solution.py:443
  3.3 0.5 collective-permute-start
  4.4 1.0 bitcast_select_fusion
  6.0 2.9 %collective-permute-start.5 = (bf16[256,128]{1,0:T(8,128)(2,1)S(1)}, bf16[256,128]{1,0:T(8,128)(2,1)S(1)}, u32[]{:S(2)}, u32[]{:S(2)}) collective-permute-start(bf16[256,128]{1,0:T(8,128)(2,1)S(1)} %get-tuple-element.24), channel_id=1, source_target_pairs={{0,3},{1,0},{2,1},{3,2},{4,7},{5,4},{6,5},{7,6},{8,11},{9,8},{10,9... | collective-permute-start | bytes 196616 | tf_op jit(solution)/shard_map/ppermute | solution.py:443
  8.9 0.6 collective-permute-start.4
  9.4 1.2 %multiply_convert_fusion.refs_3_.refs_8_ = bf16[256,2048]{1,0:T(8,128)(2,1)} fusion(bf16[256,2048]{1,0:T(8,128)(2,1)S(1)} %copy-done, f32[2048]{0:T(1024)S(1)} %add_multiply_fusion), kind=kLoop, calls=%fused_computation | loop fusion | flops 1572864 | bytes 2105344 | tf_op jit(solution)/shard_map/convert_element_type | solution.py:482
  10.7 0.6 broadcast_multiply_fusion
  11.3 1.5 %collective-permute-done.5 = bf16[256,128]{1,0:T(8,128)(2,1)S(1)} collective-permute-done((bf16[256,128]{1,0:T(8,128)(2,1)S(1)}, bf16[256,128]{1,0:T(8,128)(2,1)S(1)}, u32[]{:S(2)}, u32[]{:S(2)}) %collective-permute-start.5) | collective-permute-done | bytes 65568 | tf_op jit(solution)/shard_map/ppermute | solution.py:443
  12.8 4.6 %collective-permute-start.3 = (bf16[256,128]{1,0:T(8,128)(2,1)S(1)}, bf16[256,128]{1,0:T(8,128)(2,1)S(1)}, u32[]{:S(2)}, u32[]{:S(2)}) collective-permute-start(bf16[256,128]{1,0:T(8,128)(2,1)S(1)} %get-tuple-element.26), channel_id=1, source_target_pairs={{0,1},{1,2},{2,3},{3,0},{4,5},{5,6},{6,7},{7,4},{8,9},{9,10},{10,1... | collective-permute-start | bytes 196616 | tf_op jit(solution)/shard_map/ppermute | solution.py:443
  17.4 0.6 add_convert_fusion.refs_0_
  18.1 1.2 collective-permute-done.4
  19.6 3.0 %collective-permute-start.13 = (bf16[1024,128]{1,0:T(8,128)(2,1)S(1)}, bf16[1024,128]{1,0:T(8,128)(2,1)S(1)}, u32[]{:S(2)}, u32[]{:S(2)}) collective-permute-start(bf16[1024,128]{1,0:T(8,128)(2,1)S(1)} %pad_maximum_fusion.2.refs_2_), channel_id=1, source_target_pairs={{0,4},{4,0},{8,12},{12,8},{1,5},{5,1},{9,13},{13,9},{2,6},{6,2},{1... | collective-permute-start | bytes 786440 | tf_op jit(solution)/shard_map/ppermute | solution.py:446
  22.5 0.5 collective-permute-start.12
  23.0 1.0 collective-permute-start.7
  24.1 0.7 collective-permute-start.10
  24.8 0.5 collective-permute-start.8
  25.3 8.4 %collective-permute-done.7 = bf16[256,256]{1,0:T(8,128)(2,1)S(1)} collective-permute-done((bf16[256,256]{1,0:T(8,128)(2,1)S(1)}, bf16[256,256]{1,0:T(8,128)(2,1)S(1)}, u32[]{:S(2)}, u32[]{:S(2)}) %collective-permute-start.7) | collective-permute-done | bytes 131104 | tf_op jit(solution)/shard_map/ppermute | solution.py:446
  33.7 0.5 collective-permute-start.9
  34.2 2.3 %collective-permute-done.8 = bf16[256,256]{1,0:T(8,128)(2,1)S(1)} collective-permute-done((bf16[256,256]{1,0:T(8,128)(2,1)S(1)}, bf16[256,256]{1,0:T(8,128)(2,1)S(1)}, u32[]{:S(2)}, u32[]{:S(2)}) %collective-permute-start.8) | collective-permute-done | bytes 131104 | tf_op jit(solution)/shard_map/ppermute | solution.py:446
  36.5 2.0 %collective-permute-done.9 = bf16[256,256]{1,0:T(8,128)(2,1)S(1)} collective-permute-done((bf16[256,256]{1,0:T(8,128)(2,1)S(1)}, bf16[256,256]{1,0:T(8,128)(2,1)S(1)}, u32[]{:S(2)}, u32[]{:S(2)}) %collective-permute-start.9) | collective-permute-done | bytes 131104 | tf_op jit(solution)/shard_map/ppermute | solution.py:446
  38.6 1.7 %collective-permute-start.11 = (bf16[1024,256]{1,0:T(8,128)(2,1)S(1)}, bf16[1024,256]{1,0:T(8,128)(2,1)S(1)}, u32[]{:S(2)}, u32[]{:S(2)}) collective-permute-start(bf16[1024,256]{1,0:T(8,128)(2,1)S(1)} %constant_dynamic-update-slice_fusion.refs_2_), channel_id=1, source_target_pairs={{0,4},{4,0},{8,12},{12,8},{1,5},{5,1},{9,13},{13,9},{2,6},{6,2},{1... | collective-permute-start | bytes 1572872 | tf_op jit(solution)/shard_map/ppermute | solution.py:446
  40.4 11.0 %shard_map.64 = (bf16[1024,2048]{1,0:T(8,128)(2,1)}, bf16[1024,2048]{1,0:T(8,128)(2,1)}, f32[80,2048]{1,0:T(8,128)}, f32[4,8,256]{2,1,0:T(8,128)}, s32[2]{0:T(128)}) custom-call(s32[1]{0:T(128)} %constant.58.clone.1.refs_0_, bf16[1024,256]{1,0:T(8,128)(2,1)} %copy-done.4, bf16[1024,128]{1,0:T(8,128)(2,1)} %copy-done.8, ...), custom_call_target="tpu_custom_call" | custom-call | flops 10000000000 | bytes 50000000 | tf_op jit(solution)/shard_map/pallas_call | solution.py:490
  51.5 0.6 copy-done.5
  52.6 46.6 %shard_map.65 = (f32[64,2048]{1,0:T(8,128)}, f32[64,2048]{1,0:T(8,128)}, f32[64,2048]{1,0:T(8,128)}, f32[16]{0:T(128)}) custom-call(s32[3]{0:T(128)} %add_convert_fusion.refs_0_, s32[2]{0:T(128)} %get-tuple-element.14.refs_1_, bf16[1024,256]{1,0:T(8,128)(2,1)} %copy-done.1, bf16[1024,256]{1,0:T(8,128)(2,1)} %copy-done.2, bf16[1024,256]{1,0:T(8,128)(2,1)} %copy-done.3, ...), custom_call_target="tpu_custom_call" | custom-call | tf_op jit(solution)/shard_map/pallas_call | solution.py:515
  99.2 3.4 %collective-permute-start.17 = (f32[16]{0:T(128)}, f32[16]{0:T(128)S(1)}, u32[]{:S(2)}, u32[]{:S(2)}) collective-permute-start(f32[16]{0:T(128)} %get-tuple-element.19.refs_0_), channel_id=1, source_target_pairs={{0,3},{1,0},{2,1},{3,2},{4,7},{5,4},{6,5},{7,6},{8,11},{9,8},{10,9... | collective-permute-start | bytes 200 | tf_op jit(solution)/shard_map/ppermute | solution.py:443
  102.9 0.4 collective-permute-done.17.refs_3_
  103.4 2.9 %collective-permute-done.16.refs_2_ = f32[16]{0:T(128)S(1)} collective-permute-done((f32[16]{0:T(128)}, f32[16]{0:T(128)S(1)}, u32[]{:S(2)}, u32[]{:S(2)}) %collective-permute-start.16) | collective-permute-done | bytes 96 | tf_op jit(solution)/shard_map/ppermute | solution.py:443
  106.3 0.8 collective-permute-done.15.refs_1_
  107.1 0.5 copy-done.14
  107.6 2.3 %shard_map.66 = f32[4,64,512]{2,1,0:T(8,128)} custom-call(f32[16]{0:T(128)} %get-tuple-element.19.refs_0_, f32[16]{0:T(128)} %copy-done.14, f32[16]{0:T(128)} %copy-done.13, f32[16]{0:T(128)} %copy-done.12, f32[64,2048]{1,0:T(8,128)} %get-tuple-element.20.refs_4_, f32[64,2048]{1,0:T(8,128)} %get-tuple-element.21.refs_5_, f32[64,2048]{1,0:T(8,128)} %get-tuple-element.22.refs_6_), custom_call_target="tpu_custom_call" | custom-call | tf_op jit(solution)/shard_map/pallas_call | solution.py:540
  109.9 12.6 %all_to_all.5 = f32[4,64,512]{2,1,0:T(8,128)S(1)} all-to-all(f32[4,64,512]{2,1,0:T(8,128)} %shard_map.66), channel_id=1, replica_groups=mesh['grp'=2,'epoch'=4,'asset'=4] {'asset'}, dimensions={0} | all-to-all | bytes 1048576 | tf_op jit(solution)/shard_map/all_to_all | solution.py:547
  122.5 1.0 copy.7
  (59 shorter events, 1.8 us)
Async XLA Ops:
  0.0 9.4 %copy-start.10 = (s32[2048]{0:T(1024)S(1)}, s32[2048]{0:T(1024)}, u32[]{:S(2)}) copy-start(s32[2048]{0:T(1024)} %param.11) | copy-start | bytes 24580
  0.0 9.4 %copy-start = (bf16[256,2048]{1,0:T(8,128)(2,1)S(1)}, bf16[256,2048]{1,0:T(8,128)(2,1)}, u32[]{:S(2)}) copy-start(bf16[256,2048]{1,0:T(8,128)(2,1)} %param.9) | copy-start | bytes 3145732
  0.0 22.5 %collective-permute-start.2 = (bf16[256,256]{1,0:T(8,128)(2,1)}, bf16[256,256]{1,0:T(8,128)(2,1)S(1)}, u32[]{:S(2)}, u32[]{:S(2)}) collective-permute-start(bf16[256,256]{1,0:T(8,128)(2,1)} %bitcast.31), channel_id=1, source_target_pairs={{0,3},{1,0},{2,1},{3,2},{4,7},{5,4},{6,5},{7,6},{8,11},{9,8},{10,9... | collective-permute-start | bytes 393224 | tf_op jit(solution)/shard_map/ppermute | solution.py:443
  3.3 20.7 %collective-permute-start.1 = (bf16[256,256]{1,0:T(8,128)(2,1)}, bf16[256,256]{1,0:T(8,128)(2,1)S(1)}, u32[]{:S(2)}, u32[]{:S(2)}) collective-permute-start(bf16[256,256]{1,0:T(8,128)(2,1)} %bitcast.32), channel_id=1, source_target_pairs={{0,2},{1,3},{2,0},{3,1},{4,6},{5,7},{6,4},{7,5},{8,10},{9,11},{10,... | collective-permute-start | bytes 393224 | tf_op jit(solution)/shard_map/ppermute | solution.py:443
  3.3 19.7 %collective-permute-start = (bf16[256,256]{1,0:T(8,128)(2,1)}, bf16[256,256]{1,0:T(8,128)(2,1)S(1)}, u32[]{:S(2)}, u32[]{:S(2)}) collective-permute-start(bf16[256,256]{1,0:T(8,128)(2,1)} %bitcast.33), channel_id=1, source_target_pairs={{0,1},{1,2},{2,3},{3,0},{4,5},{5,6},{6,7},{7,4},{8,9},{9,10},{10,1... | collective-permute-start | bytes 393224 | tf_op jit(solution)/shard_map/ppermute | solution.py:443
  5.5 5.2 %copy-start.11 = (f32[2048]{0:T(1024)S(1)}, f32[2048]{0:T(1024)}, u32[]{:S(2)}) copy-start(f32[2048]{0:T(1024)} %param.10) | copy-start | bytes 24580
  5.6 13.7 %copy-start.9 = (bf16[1,256,256]{2,1,0:T(8,128)(2,1)S(1)}, bf16[1,256,256]{2,1,0:T(8,128)(2,1)}, u32[]{:S(2)}) copy-start(bf16[1,256,256]{2,1,0:T(8,128)(2,1)} %param.6) | copy-start | bytes 393220
  6.0 6.8 %collective-permute-start.5 = (bf16[256,128]{1,0:T(8,128)(2,1)S(1)}, bf16[256,128]{1,0:T(8,128)(2,1)S(1)}, u32[]{:S(2)}, u32[]{:S(2)}) collective-permute-start(bf16[256,128]{1,0:T(8,128)(2,1)S(1)} %get-tuple-element.24), channel_id=1, source_target_pairs={{0,3},{1,0},{2,1},{3,2},{4,7},{5,4},{6,5},{7,6},{8,11},{9,8},{10,9... | collective-permute-start | bytes 196616 | tf_op jit(solution)/shard_map/ppermute | solution.py:443
  8.9 10.4 %collective-permute-start.4 = (bf16[256,128]{1,0:T(8,128)(2,1)S(1)}, bf16[256,128]{1,0:T(8,128)(2,1)S(1)}, u32[]{:S(2)}, u32[]{:S(2)}) collective-permute-start(bf16[256,128]{1,0:T(8,128)(2,1)S(1)} %get-tuple-element.25), channel_id=1, source_target_pairs={{0,2},{1,3},{2,0},{3,1},{4,6},{5,7},{6,4},{7,5},{8,10},{9,11},{10,... | collective-permute-start | bytes 196616 | tf_op jit(solution)/shard_map/ppermute | solution.py:443
  12.8 6.7 %collective-permute-start.3 = (bf16[256,128]{1,0:T(8,128)(2,1)S(1)}, bf16[256,128]{1,0:T(8,128)(2,1)S(1)}, u32[]{:S(2)}, u32[]{:S(2)}) collective-permute-start(bf16[256,128]{1,0:T(8,128)(2,1)S(1)} %get-tuple-element.26), channel_id=1, source_target_pairs={{0,1},{1,2},{2,3},{3,0},{4,5},{5,6},{6,7},{7,4},{8,9},{9,10},{10,1... | collective-permute-start | bytes 196616 | tf_op jit(solution)/shard_map/ppermute | solution.py:443
  19.3 5.5 %collective-permute-start.6 = (bf16[256,256]{1,0:T(8,128)(2,1)S(1)}, bf16[256,256]{1,0:T(8,128)(2,1)S(1)}, u32[]{:S(2)}, u32[]{:S(2)}) collective-permute-start(bf16[256,256]{1,0:T(8,128)(2,1)S(1)} %bitcast.34), channel_id=1, source_target_pairs={{0,8},{4,12},{8,0},{12,4},{1,9},{5,13},{9,1},{13,5},{2,10},{6,14},... | collective-permute-start | bytes 393224 | tf_op jit(solution)/shard_map/ppermute | solution.py:446
  19.6 20.8 %copy-start.8 = (bf16[1024,128]{1,0:T(8,128)(2,1)}, bf16[1024,128]{1,0:T(8,128)(2,1)S(1)}, u32[]{:S(2)}) copy-start(bf16[1024,128]{1,0:T(8,128)(2,1)S(1)} %pad_maximum_fusion.2.refs_2_) | copy-start | bytes 786436
  19.6 31.8 %collective-permute-start.13 = (bf16[1024,128]{1,0:T(8,128)(2,1)S(1)}, bf16[1024,128]{1,0:T(8,128)(2,1)S(1)}, u32[]{:S(2)}, u32[]{:S(2)}) collective-permute-start(bf16[1024,128]{1,0:T(8,128)(2,1)S(1)} %pad_maximum_fusion.2.refs_2_), channel_id=1, source_target_pairs={{0,4},{4,0},{8,12},{12,8},{1,5},{5,1},{9,13},{13,9},{2,6},{6,2},{1... | collective-permute-start | bytes 786440 | tf_op jit(solution)/shard_map/ppermute | solution.py:446
  22.5 17.8 %collective-permute-start.12 = (bf16[1024,128]{1,0:T(8,128)(2,1)S(1)}, bf16[1024,128]{1,0:T(8,128)(2,1)S(1)}, u32[]{:S(2)}, u32[]{:S(2)}) collective-permute-start(bf16[1024,128]{1,0:T(8,128)(2,1)S(1)} %pad_maximum_fusion.2.refs_2_), channel_id=1, source_target_pairs={{0,8},{4,12},{8,0},{12,4},{1,9},{5,13},{9,1},{13,5},{2,10},{6,14},... | collective-permute-start | bytes 786440 | tf_op jit(solution)/shard_map/ppermute | solution.py:446
  23.0 10.6 %collective-permute-start.7 = (bf16[256,256]{1,0:T(8,128)(2,1)S(1)}, bf16[256,256]{1,0:T(8,128)(2,1)S(1)}, u32[]{:S(2)}, u32[]{:S(2)}) collective-permute-start(bf16[256,256]{1,0:T(8,128)(2,1)S(1)} %collective-permute-done), channel_id=1, source_target_pairs={{0,8},{4,12},{8,0},{12,4},{1,9},{5,13},{9,1},{13,5},{2,10},{6,14},... | collective-permute-start | bytes 393224 | tf_op jit(solution)/shard_map/ppermute | solution.py:446
  24.0 16.3 %copy-start.4 = (bf16[1024,256]{1,0:T(8,128)(2,1)}, bf16[1024,256]{1,0:T(8,128)(2,1)S(1)}, u32[]{:S(2)}) copy-start(bf16[1024,256]{1,0:T(8,128)(2,1)S(1)} %pad_maximum_fusion.refs_1_) | copy-start | bytes 1572868
  24.1 27.4 %collective-permute-start.10 = (bf16[1024,256]{1,0:T(8,128)(2,1)S(1)}, bf16[1024,256]{1,0:T(8,128)(2,1)S(1)}, u32[]{:S(2)}, u32[]{:S(2)}) collective-permute-start(bf16[1024,256]{1,0:T(8,128)(2,1)S(1)} %pad_maximum_fusion.refs_1_), channel_id=1, source_target_pairs={{0,4},{4,0},{8,12},{12,8},{1,5},{5,1},{9,13},{13,9},{2,6},{6,2},{1... | collective-permute-start | bytes 1572872 | tf_op jit(solution)/shard_map/ppermute | solution.py:446
  24.8 11.7 %collective-permute-start.8 = (bf16[256,256]{1,0:T(8,128)(2,1)S(1)}, bf16[256,256]{1,0:T(8,128)(2,1)S(1)}, u32[]{:S(2)}, u32[]{:S(2)}) collective-permute-start(bf16[256,256]{1,0:T(8,128)(2,1)S(1)} %collective-permute-done.1), channel_id=1, source_target_pairs={{0,8},{4,12},{8,0},{12,4},{1,9},{5,13},{9,1},{13,5},{2,10},{6,14},... | collective-permute-start | bytes 393224 | tf_op jit(solution)/shard_map/ppermute | solution.py:446
  33.7 4.9 %collective-permute-start.9 = (bf16[256,256]{1,0:T(8,128)(2,1)S(1)}, bf16[256,256]{1,0:T(8,128)(2,1)S(1)}, u32[]{:S(2)}, u32[]{:S(2)}) collective-permute-start(bf16[256,256]{1,0:T(8,128)(2,1)S(1)} %collective-permute-done.2), channel_id=1, source_target_pairs={{0,8},{4,12},{8,0},{12,4},{1,9},{5,13},{9,1},{13,5},{2,10},{6,14},... | collective-permute-start | bytes 393224 | tf_op jit(solution)/shard_map/ppermute | solution.py:446
  38.5 12.8 %copy-start.1 = (bf16[1024,256]{1,0:T(8,128)(2,1)}, bf16[1024,256]{1,0:T(8,128)(2,1)S(1)}, u32[]{:S(2)}) copy-start(bf16[1024,256]{1,0:T(8,128)(2,1)S(1)} %constant_dynamic-update-slice_fusion.refs_2_) | copy-start | bytes 1572868
  38.6 12.9 %collective-permute-start.11 = (bf16[1024,256]{1,0:T(8,128)(2,1)S(1)}, bf16[1024,256]{1,0:T(8,128)(2,1)S(1)}, u32[]{:S(2)}, u32[]{:S(2)}) collective-permute-start(bf16[1024,256]{1,0:T(8,128)(2,1)S(1)} %constant_dynamic-update-slice_fusion.refs_2_), channel_id=1, source_target_pairs={{0,4},{4,0},{8,12},{12,8},{1,5},{5,1},{9,13},{13,9},{2,6},{6,2},{1... | collective-permute-start | bytes 1572872 | tf_op jit(solution)/shard_map/ppermute | solution.py:446
  40.3 11.1 %copy-start.6 = (bf16[1024,128]{1,0:T(8,128)(2,1)}, bf16[1024,128]{1,0:T(8,128)(2,1)S(1)}, u32[]{:S(2)}) copy-start(bf16[1024,128]{1,0:T(8,128)(2,1)S(1)} %collective-permute-done.12.refs_5_) | copy-start | bytes 786436
  40.3 11.1 %collective-permute-start.14 = (bf16[1024,128]{1,0:T(8,128)(2,1)S(1)}, bf16[1024,128]{1,0:T(8,128)(2,1)S(1)}, u32[]{:S(2)}, u32[]{:S(2)}) collective-permute-start(bf16[1024,128]{1,0:T(8,128)(2,1)S(1)} %collective-permute-done.12.refs_5_), channel_id=1, source_target_pairs={{0,4},{4,0},{8,12},{12,8},{1,5},{5,1},{9,13},{13,9},{2,6},{6,2},{1... | collective-permute-start | bytes 786440 | tf_op jit(solution)/shard_map/ppermute | solution.py:446
  51.4 0.7 copy-start.5
  51.4 0.8 copy-start.7
  51.4 0.9 copy-start.2
  51.5 1.1 copy-start.3
  99.2 4.2 %collective-permute-start.17 = (f32[16]{0:T(128)}, f32[16]{0:T(128)S(1)}, u32[]{:S(2)}, u32[]{:S(2)}) collective-permute-start(f32[16]{0:T(128)} %get-tuple-element.19.refs_0_), channel_id=1, source_target_pairs={{0,3},{1,0},{2,1},{3,2},{4,7},{5,4},{6,5},{7,6},{8,11},{9,8},{10,9... | collective-permute-start | bytes 200 | tf_op jit(solution)/shard_map/ppermute | solution.py:443
  102.6 3.7 %collective-permute-start.16 = (f32[16]{0:T(128)}, f32[16]{0:T(128)S(1)}, u32[]{:S(2)}, u32[]{:S(2)}) collective-permute-start(f32[16]{0:T(128)} %get-tuple-element.19.refs_0_), channel_id=1, source_target_pairs={{0,2},{1,3},{2,0},{3,1},{4,6},{5,7},{6,4},{7,5},{8,10},{9,11},{10,... | collective-permute-start | bytes 200 | tf_op jit(solution)/shard_map/ppermute | solution.py:443
  102.6 4.5 %collective-permute-start.15 = (f32[16]{0:T(128)}, f32[16]{0:T(128)S(1)}, u32[]{:S(2)}, u32[]{:S(2)}) collective-permute-start(f32[16]{0:T(128)} %get-tuple-element.19.refs_0_), channel_id=1, source_target_pairs={{0,1},{1,2},{2,3},{3,0},{4,5},{5,6},{6,7},{7,4},{8,9},{9,10},{10,1... | collective-permute-start | bytes 200 | tf_op jit(solution)/shard_map/ppermute | solution.py:443
  103.4 3.7 %copy-start.12 = (f32[16]{0:T(128)}, f32[16]{0:T(128)S(1)}, u32[]{:S(2)}) copy-start(f32[16]{0:T(128)S(1)} %collective-permute-done.17.refs_3_) | copy-start | bytes 196
  106.3 0.8 copy-start.13
  (1 other events, 0.5 us)
